TPU v7x, 768 devices: a whole 4x8x12 slice. The times are simulated.
768 devices in a mesh: replica: 48 (over x_lo, z, core), fsdp: 16 (over x_hi, y).
Axes of the slice: x: 4 (x_hi: 2, x_lo: 2; x = x_hi * 2 + x_lo), y: 8, z: 12, core: 2. Of those that a mesh axis runs over, the one named last changes fastest.
Arguments:
- hidden_in: bfloat16 [98304, 4096], P(('replica', 'fsdp')), may hold values from -60 to 60
- res_grad: bfloat16 [98304, 4096], P(('replica', 'fsdp')), may hold values from -0.59765625 to 0.59765625
- value_grad: bfloat16 [98304, 512], P(('replica', 'fsdp')), may hold values from -1.5 to 1.5
- value_weight: bfloat16 [48, 4096, 512], P('replica', 'fsdp'), may hold values from -0.09375 to 0.09375
- norm_gain: float32 [48, 4096], P('replica'), may hold values from 0.5 to 1.5
- inner_frag: float32 [48, 4096, 768], P('replica', 'fsdp'), may hold values from -6 to 6
- outer_frag: float32 [4096, 768], P('fsdp'), may hold values from -6 to 6
- momentum: float32 [4096, 768], P('fsdp'), may hold values from -3 to 3
Outputs:
- hidden_grad: bfloat16 [98304, 4096], P(('replica', 'fsdp'))
- weight_grad: bfloat16 [48, 4096, 512], P('replica', 'fsdp')
- gain_grad: float32 [48, 4096], P('replica', 'fsdp')
- new_outer: float32 [4096, 768], P('fsdp')
- new_momentum: float32 [4096, 768], P('fsdp')
All inputs are finite; a program needn't handle non-finite values.
Results may differ from a plain program's by a relative error of at most 0.015.
Values may be sent and summed in bfloat16 or wider, within the bound.
No kernel may reach another device: no remote copies, remote signals or barrier semaphores. Data moves between devices by JAX's collectives and lax.ppermute only.
A program may use at most 64 MiB of HBM per device.

v0:
```python
import jax
import jax.numpy as jnp
from jax import lax
from jax.sharding import PartitionSpec as P


def body(
    hidden_in, res_grad, value_grad, value_weight, norm_gain, inner_frag, outer_frag, momentum
):
    pseudo_grad = outer_frag - inner_frag[0]
    summed = lax.psum(pseudo_grad, "replica")
    average = summed / lax.axis_size("replica")
    new_momentum = 0.9 * momentum + average
    new_outer = outer_frag - 0.7 * (average + 0.9 * new_momentum)
    widened = hidden_in.astype(jnp.float32)
    inverse = lax.rsqrt(jnp.mean(widened * widened, axis=1, keepdims=True) + 1e-05)
    unit_rows = widened * inverse
    scales = norm_gain[0]
    normed = (unit_rows * scales).astype(jnp.bfloat16)
    input_grad = lax.dot_general(
        value_grad,
        lax.all_gather(value_weight[0], "fsdp", axis=0, tiled=True),
        (((1,), (1,)), ((), ())),
        preferred_element_type=jnp.float32,
    )
    partial_gain = jnp.sum(input_grad * unit_rows, axis=0)
    row_share = value_weight.shape[1]
    gain_sum = lax.psum(partial_gain, "fsdp")
    gain_grad = lax.dynamic_slice_in_dim(gain_sum, lax.axis_index("fsdp") * row_share, row_share, 0)
    scaled = input_grad * scales
    projection = jnp.mean(scaled * unit_rows, axis=1, keepdims=True)
    hidden_grad = (
        res_grad.astype(jnp.float32) + inverse * (scaled - unit_rows * projection)
    ).astype(jnp.bfloat16)
    weight_grad = lax.psum_scatter(
        lax.dot_general(
            normed, value_grad, (((0,), (0,)), ((), ())), preferred_element_type=jnp.float32
        ).astype(jnp.bfloat16),
        "fsdp",
        scatter_dimension=0,
        tiled=True,
    )
    return (hidden_grad, weight_grad[None], gain_grad[None], new_outer, new_momentum)


def solution(mesh):
    in_specs = (
        P(("replica", "fsdp"), None),
        P(("replica", "fsdp"), None),
        P(("replica", "fsdp"), None),
        P("replica", "fsdp", None),
        P("replica", None),
        P("replica", "fsdp", None),
        P("fsdp", None),
        P("fsdp", None),
    )
    out_specs = (
        P(("replica", "fsdp"), None),
        P("replica", "fsdp", None),
        P("replica", "fsdp"),
        P("fsdp", None),
        P("fsdp", None),
    )
    return jax.shard_map(body, mesh=mesh, in_specs=in_specs, out_specs=out_specs, check_vma=False)
```

profile of v0, /device:TPU:2, one launch (start us, length us, event | category | flops | bytes accessed | tf_op | source)
XLA Modules:
  0.0 453.7 jit_solution(14079887302787187966)
XLA Ops:
  8.0 0.0 copy-start
  8.0 0.0 copy-start.1
  8.0 0.0 copy-start.4
  8.0 0.0 all-reduce.2.cloned.1.call-start
  8.1 2.4 bitcast_subtract_fusion
  10.5 0.0 all-reduce.2.cloned.1.call-update
  10.5 0.0 all-gather.3.cloned.1.call-start
  10.6 0.5 all-gather.3.cloned.1.call-update
  11.1 0.0 reduce-scatter.2.cloned.1.call-start
  11.2 0.0 copy-done.1
  11.2 0.3 fusion.13
  11.5 0.0 copy-done
  11.5 0.0 copy-done.4
  11.5 3.3 convolution_convert_fusion
  14.8 0.0 copy-start.2
  14.8 0.0 copy-start.3
  14.8 0.0 reduce-scatter.2.cloned.1.call-update
  14.9 345.7 %all-reduce.2.cloned.1.call-done = f32[256,768]{1,0:T(8,128)} async-done(((f32[256,768]{1,0:T(8,128)}), f32[256,768]{1,0:T(8,128)}) %all-reduce.2.cloned.1.call-update) | async-done | bytes 786448 | tf_op jit(solution)/shard_map/psum | solution.py:11
  360.6 0.0 copy-done.2
  360.6 0.0 copy-done.3
  360.6 2.5 multiply_subtract_fusion
  363.1 0.0 all-gather.3.cloned.1.call-done
  363.1 3.8 fusion.12
  366.9 75.9 %psum.14 = f32[4096]{0:T(1024)S(1)} all-reduce(f32[4096]{0:T(1024)S(1)} %get-tuple-element.5), channel_id=1, replica_groups=mesh['replica'=48,'fsdp'=16] {'fsdp'}, use_global_device_ids=true, to_apply=%region_4.0 | all-reduce | flops 4096 | bytes 32768 | tf_op jit(solution)/shard_map/psum | solution.py:28
  442.8 0.6 dynamic_slice.3
  443.4 2.9 fusion.10
  446.3 0.0 reduce-scatter.2.cloned.1.call-done
  (2 shorter events, 0.0 us)
Async XLA Ops:
  8.0 3.5 copy-start
  8.0 3.1 copy-start.1
  8.0 3.4 copy-start.4
  8.0 352.5 %all-reduce.2.cloned.1.call-start = ((), (), s32[]{:S(2)}) async-start(), calls=%async_computation.2 | async-start | bytes 1572864 | tf_op jit(solution)/shard_map/psum | solution.py:11
  10.5 352.5 %all-gather.3.cloned.1.call-start = ((), (), s32[]{:S(2)}) async-start(), calls=%async_computation.3 | async-start | bytes 4456448 | tf_op jit(solution)/shard_map/all_gather | solution.py:22
  11.1 435.2 %reduce-scatter.2.cloned.1.call-start = ((), (), s32[]{:S(2)}) async-start(), calls=%async_computation.1 | async-start | bytes 4456448 | tf_op jit(solution)/shard_map/reduce_scatter | solution.py:35
  14.8 345.7 %copy-start.2 = (f32[256,768]{1,0:T(8,128)S(1)}, f32[256,768]{1,0:T(8,128)}, u32[]{:S(2)}) copy-start(f32[256,768]{1,0:T(8,128)} %param.14) | copy-start | bytes 2359300
  14.8 345.7 %copy-start.3 = (f32[256,768]{1,0:T(8,128)S(1)}, f32[256,768]{1,0:T(8,128)}, u32[]{:S(2)}) copy-start(f32[256,768]{1,0:T(8,128)} %param.15) | copy-start | bytes 2359300
Sparse Core Ops, SparseCore 0:
  12.6 347.9 all-reduce.1
Sparse Core Ops, SparseCore 1:
  14.8 116.9 all-gather.2
  137.3 217.8 reduce-scatter.1
where the time goes:
time: 454 us
  waiting for transfers between devices  346 us (76%)
  blocking collectives  75.9 us (17%)
  between operations  15.5 us (3%)
  other arithmetic  8.09 us (2%)
  matrix products  7.13 us (2%)
    psum x1, waiting for transfers between devices, body(): summed = lax.psum(pseudo_grad, 'replica')  346 us
    psum x1, blocking collectives, body(): gain_sum = lax.psum(partial_gain, 'fsdp')  75.9 us
  transfers between devices with their start and end apart: 3, of which 1 were waited for; matrix products, arithmetic and copies ran while one was open for 3% of the time, Pallas kernels for 0%

commit v1 on v0

v1 whole, which is shorter than its diff:
```python
import jax
import jax.numpy as jnp
from jax import lax
from jax.experimental import pallas as pl
from jax.experimental.pallas import tpu as pltpu
from jax.sharding import Mesh, PartitionSpec as P


AXES = ("x_lo", "z", "core", "x_hi", "y")
REPLICA = AXES[:3]
FSDP = AXES[3:]
SWAP = [(0, 1), (1, 0)]
f32, bf16 = jnp.float32, jnp.bfloat16
ROWS = 16


def whole():
    return pl.BlockSpec(memory_space=pltpu.VMEM)


def scalar():
    return pl.BlockSpec(memory_space=pltpu.SMEM)


def call(kernel, out_shape, operands, flops=0):
    outs = out_shape if isinstance(out_shape, (tuple, list)) else (out_shape,)
    moved = sum(a.size * a.dtype.itemsize for a in (*operands, *outs))
    return pl.pallas_call(
        kernel,
        out_shape=out_shape,
        in_specs=[scalar() if a.dtype == jnp.int32 else whole() for a in operands],
        out_specs=jax.tree.map(lambda _: whole(), out_shape),
        cost_estimate=pl.CostEstimate(flops=flops, bytes_accessed=moved, transcendentals=0),
    )(*operands)


def shape(dims, dtype):
    return jax.ShapeDtypeStruct(dims, dtype)


def inverse_of(rows):
    return lax.rsqrt(jnp.mean(rows * rows, axis=1, keepdims=True) + 1e-05)


def norm_kernel(upper_ref, hidden_ref, scales_ref, kept_ref, sent_ref):
    tokens, width = hidden_ref.shape
    half = width // 2
    own = pl.multiple_of(upper_ref[0] * half, half)
    other = pl.multiple_of((1 - upper_ref[0]) * half, half)

    def step(index, _):
        at = pl.ds(pl.multiple_of(index * ROWS, ROWS), ROWS)
        inverse = inverse_of(hidden_ref[at, :].astype(f32))
        for start, target in ((other, sent_ref), (own, kept_ref)):
            columns = pl.ds(start, half)
            unit = hidden_ref[at, columns].astype(f32) * inverse
            target[at, :] = (unit * scales_ref[:, columns]).astype(bf16)
        return 0

    lax.fori_loop(0, tokens // ROWS, step, 0)


def pseudo_kernel(outer_ref, inner_ref, out_ref):
    for at in range(out_ref.shape[0]):
        columns = slice(at * 128, (at + 1) * 128)
        out_ref[at] = (outer_ref[:, columns] - inner_ref[:, columns]).astype(bf16)


def block_kernel(spread_ref, out_ref):
    count = spread_ref.shape[0]
    total = spread_ref[0].astype(f32)
    for at in range(1, count):
        total += spread_ref[at].astype(f32)
    mean = (total / count).astype(bf16)
    for at in range(count):
        out_ref[at] = mean


def outer_kernel(shared_ref, outer_ref, momentum_ref, new_outer_ref, new_momentum_ref):
    for at in range(shared_ref.shape[0]):
        columns = slice(at * 128, (at + 1) * 128)
        average = shared_ref[at].astype(f32)
        new_momentum = 0.9 * momentum_ref[:, columns] + average
        new_momentum_ref[:, columns] = new_momentum
        new_outer_ref[:, columns] = outer_ref[:, columns] - 0.7 * (average + 0.9 * new_momentum)


def hidden_kernel(upper_ref, hidden_ref, res_ref, scales_ref, own_ref, other_ref, out_ref):
    tokens, width = hidden_ref.shape
    half = width // 2
    own = pl.multiple_of(upper_ref[0] * half, half)
    other = pl.multiple_of((1 - upper_ref[0]) * half, half)

    def step(index, _):
        at = pl.ds(pl.multiple_of(index * ROWS, ROWS), ROWS)
        inverse = inverse_of(hidden_ref[at, :].astype(f32))
        total = jnp.zeros((ROWS, 1), f32)
        parts = ((own, own_ref), (other, other_ref))
        for start, grad_ref in parts:
            columns = pl.ds(start, half)
            scaled = grad_ref[at, :].astype(f32) * scales_ref[:, columns]
            unit = hidden_ref[at, columns].astype(f32) * inverse
            total += jnp.sum(scaled * unit, axis=1, keepdims=True)
        projection = total / width
        for start, grad_ref in parts:
            columns = pl.ds(start, half)
            scaled = grad_ref[at, :].astype(f32) * scales_ref[:, columns]
            unit = hidden_ref[at, columns].astype(f32) * inverse
            grad = res_ref[at, columns].astype(f32) + inverse * (scaled - unit * projection)
            out_ref[at, columns] = grad.astype(bf16)
        return 0

    lax.fori_loop(0, tokens // ROWS, step, 0)


def body(
    hidden_in, res_grad, value_grad, value_weight, norm_gain, inner_frag, outer_frag, momentum
):
    upper = lax.axis_index("x_hi").reshape(1)
    own_weight = value_weight[0]
    tokens, width = hidden_in.shape
    half = width // 2
    weight_half = lax.all_gather(own_weight, "y", axis=0, tiled=True)
    partner_value = lax.ppermute(value_grad, "x_hi", SWAP)

    kept, sent = call(
        norm_kernel,
        (shape((tokens, half), bf16), shape((tokens, half), bf16)),
        (upper, hidden_in, norm_gain),
    )
    received = lax.ppermute(sent, "x_hi", SWAP)
    term = lax.dot_general(
        jnp.concatenate([kept, received], axis=0),
        jnp.concatenate([value_grad, partner_value], axis=0),
        (((0,), (0,)), ((), ())),
        preferred_element_type=f32,
    ).astype(bf16)
    weight_grad = lax.psum_scatter(term, "y", scatter_dimension=0, tiled=True)

    rows, columns = outer_frag.shape
    split = (columns // 128, rows, 128)
    pseudo_grad = call(
        pseudo_kernel, shape(split, bf16), (outer_frag, inner_frag[0])
    ).reshape(48, -1, 128)
    spread = lax.all_to_all(pseudo_grad, REPLICA, 0, 0)
    block = call(block_kernel, shape(spread.shape, bf16), (spread,))
    shared = lax.all_to_all(block, REPLICA, 0, 0)
    new_outer, new_momentum = call(
        outer_kernel,
        (shape(outer_frag.shape, f32), shape(outer_frag.shape, f32)),
        (shared.reshape(split), outer_frag, momentum),
    )

    rows_by_rows = (((1,), (1,)), ((), ()))
    partner_grad = lax.dot_general(
        partner_value, weight_half, rows_by_rows, preferred_element_type=f32
    ).astype(bf16)
    other_grad = lax.ppermute(partner_grad, "x_hi", SWAP)
    own_grad = lax.dot_general(value_grad, weight_half, rows_by_rows, preferred_element_type=f32)
    hidden_grad = call(
        hidden_kernel,
        shape(hidden_in.shape, bf16),
        (upper, hidden_in, res_grad, norm_gain, own_grad, other_grad),
    )

    count = own_weight.shape[0]
    own_scales = lax.dynamic_slice_in_dim(norm_gain[0], lax.axis_index(FSDP) * count, count, 0)
    gain_grad = (
        jnp.sum(own_weight.astype(f32) * weight_grad.astype(f32), axis=1) / own_scales
    )
    return (hidden_grad, weight_grad[None], gain_grad[None], new_outer, new_momentum)


def solution(mesh):
    grid = Mesh(mesh.devices.reshape(2, 12, 2, 2, 8), AXES)
    in_specs = (
        P(AXES, None),
        P(AXES, None),
        P(AXES, None),
        P(REPLICA, FSDP, None),
        P(REPLICA, None),
        P(REPLICA, FSDP, None),
        P(FSDP, None),
        P(FSDP, None),
    )
    out_specs = (
        P(AXES, None),
        P(REPLICA, FSDP, None),
        P(REPLICA, FSDP),
        P(FSDP, None),
        P(FSDP, None),
    )

    def step(*arrays):
        return body(*arrays)

    step = jax.shard_map(step, mesh=grid, in_specs=in_specs, out_specs=out_specs, check_vma=False)
    return step
```

time: 454 us -> 123 us (0.27)
  the two profiles are of different devices: /device:TPU:2 before, /device:TPU:6 now
where the time goes in v1:
time: 123 us
  blocking collectives  33.8 us (27%)
  waiting for transfers between devices  28.1 us (23%)
  starting transfers between devices  19.1 us (16%)
  Pallas kernels  15.4 us (13%)
  between operations  14.1 us (11%)
  matrix products  8.4 us (7%)
  other arithmetic  2.35 us (2%)
  local copies, waits for them, and re-layouts  1.57 us (1%)
    all_to_all x1, blocking collectives, body(): spread = lax.all_to_all(pseudo_grad, REPLICA, 0, 0)  33.8 us
    pallas_call x5, Pallas kernels, call(): pl.pallas_call(kernel, out_shape=out_shape, in_specs=[scalar() if a.dtype...  15.4 us
    ppermute x1, waiting for transfers between devices, body(): partner_value = lax.ppermute(value_grad, 'x_hi', SWAP)  12.7 us
    all_to_all x1, waiting for transfers between devices, body(): shared = lax.all_to_all(block, REPLICA, 0, 0)  10.8 us
    all_to_all x1, starting transfers between devices, body(): shared = lax.all_to_all(block, REPLICA, 0, 0)  8.35 us
    ppermute x1, starting transfers between devices, body(): partner_value = lax.ppermute(value_grad, 'x_hi', SWAP)  4.03 us
    reduce_scatter x1, waiting for transfers between devices, body(): weight_grad = lax.psum_scatter(term, 'y', scatter_dimension=0, tiled=True)  3.9 us
    ppermute x1, starting transfers between devices, body(): other_grad = lax.ppermute(partner_grad, 'x_hi', SWAP)  3.31 us
  transfers between devices with their start and end apart: 6, of which 3 were waited for; matrix products, arithmetic and copies ran while one was open for 7% of the time, Pallas kernels for 13%

profile of v1, /device:TPU:6, one launch (start us, length us, event | category | flops | bytes accessed | tf_op | source)
XLA Modules:
  0.0 122.9 jit_solution(3262759821175304161)
XLA Ops:
  7.2 0.0 all-gather.3.cloned.1.call-start
  7.2 0.7 all-gather.3.cloned.1.call-update
  7.9 0.0 reduce-scatter.2.cloned.1.call-start
  8.0 3.4 %shard_map.120 = (bf16[128,2048]{1,0:T(8,128)(2,1)}, bf16[128,2048]{1,0:T(8,128)(2,1)}) custom-call(s32[1]{0:T(128)} %bitcast.upper_ref, bf16[128,4096]{1,0:T(8,128)(2,1)} %hidden_ref.3, f32[1,4096]{1,0:T(1,128)} %scales_ref.3), custom_call_target="tpu_custom_call" | custom-call | bytes 2113540 | tf_op jit(solution)/shard_map/pallas_call | solution.py:28
  11.3 3.3 %collective-permute-start.2 = (bf16[128,2048]{1,0:T(8,128)(2,1)}, bf16[128,2048]{1,0:T(8,128)(2,1)S(1)}, u32[]{:S(2)}, u32[]{:S(2)}) collective-permute-start(bf16[128,2048]{1,0:T(8,128)(2,1)} %get-tuple-element.10), channel_id=1, source_target_pairs={{0,8},{8,0},{1,9},{9,1},{2,10},{10,2},{3,11},{11,3},{4,12},{12,4},... | collective-permute-start | bytes 1572872 | tf_op jit(solution)/shard_map/ppermute | solution.py:131
  14.6 4.0 %collective-permute-start = (bf16[128,512]{1,0:T(8,128)(2,1)}, bf16[128,512]{1,0:T(8,128)(2,1)S(1)}, u32[]{:S(2)}, u32[]{:S(2)}) collective-permute-start(bf16[128,512]{1,0:T(8,128)(2,1)} %param.10), channel_id=1, source_target_pairs={{0,8},{8,0},{1,9},{9,1},{2,10},{10,2},{3,11},{11,3},{4,12},{12,4},... | collective-permute-start | bytes 393224 | tf_op jit(solution)/shard_map/ppermute | solution.py:124
  18.7 12.7 %collective-permute-done = bf16[128,512]{1,0:T(8,128)(2,1)S(1)} collective-permute-done((bf16[128,512]{1,0:T(8,128)(2,1)}, bf16[128,512]{1,0:T(8,128)(2,1)S(1)}, u32[]{:S(2)}, u32[]{:S(2)}) %collective-permute-start) | collective-permute-done | bytes 131104 | tf_op jit(solution)/shard_map/ppermute | solution.py:124
  31.4 0.0 collective-permute-done.2
  31.4 3.1 %convolution_convert_fusion = bf16[2048,512]{1,0:T(8,128)(2,1)} fusion(bf16[128,2048]{1,0:T(8,128)(2,1)S(1)} %collective-permute-done.2, bf16[128,2048]{1,0:T(8,128)(2,1)} %get-tuple-element.9, bf16[128,512]{1,0:T(8,128)(2,1)S(1)} %collective-permute-done, bf16[128,512]{1,0:T(8,128)(2,1)} %param.10), kind=kOutput, calls=%fused_computation | convolution fusion | flops 540540928 | bytes 3407872 | tf_op jit(solution)/shard_map/dot_general | solution.py:132
  34.5 0.0 reduce-scatter.2.cloned.1.call-update
  34.6 2.2 %shard_map.121 = bf16[6,256,128]{2,1,0:T(8,128)(2,1)} custom-call(f32[256,768]{1,0:T(8,128)} %outer_ref.3, f32[256,768]{1,0:T(8,128)} %bitcast.18), custom_call_target="tpu_custom_call" | custom-call | bytes 1966080 | tf_op jit(solution)/shard_map/pallas_call | solution.py:28
  36.8 33.8 %all_to_all.10.spread_ref = bf16[48,32,128]{2,1,0:T(8,128)(2,1)} all-to-all(bf16[48,32,128]{2,1,0:T(8,128)(2,1)} %bitcast.17), channel_id=1, replica_groups=mesh['x_lo'=2,'z'=12,'core'=2,'x_hi'=2,'y'=8] {'x_lo','z','core'}, dimensions={0} | all-to-all | bytes 786432 | tf_op jit(solution)/shard_map/all_to_all | solution.py:145
  70.6 1.8 %shard_map.122 = bf16[48,32,128]{2,1,0:T(8,128)(2,1)} custom-call(bf16[48,32,128]{2,1,0:T(8,128)(2,1)} %all_to_all.10.spread_ref), custom_call_target="tpu_custom_call" | custom-call | bytes 786432 | tf_op jit(solution)/shard_map/pallas_call | solution.py:28
  72.4 8.4 %all-to-all-start.1 = ((bf16[48,32,128]{2,1,0:T(8,128)(2,1)}), bf16[48,32,128]{2,1,0:T(8,128)(2,1)S(1)}, u32[]{:S(2)}, u32[]{:S(2)}) async-start(bf16[48,32,128]{2,1,0:T(8,128)(2,1)} %shard_map.122), calls=%async_computation.2 | async-start | bytes 786432 | tf_op jit(solution)/shard_map/all_to_all | solution.py:147
  80.8 0.0 all-gather.3.cloned.1.call-done
  80.8 0.0 copy-start
  80.8 2.6 %convolution_convert_fusion.1 = bf16[128,2048]{1,0:T(8,128)(2,1)S(1)} fusion(bf16[128,512]{1,0:T(8,128)(2,1)S(1)} %collective-permute-done, bf16[1,2048,512]{2,1,0:T(8,128)(2,1)} %all-gather.3.cloned.1.call-done), kind=kOutput, calls=%fused_computation.1 | convolution fusion | flops 268697600 | bytes 2752512 | tf_op jit(solution)/shard_map/dot_general | solution.py:155
  83.4 3.3 %collective-permute-start.1 = (bf16[128,2048]{1,0:T(8,128)(2,1)S(1)}, bf16[128,2048]{1,0:T(8,128)(2,1)S(1)}, u32[]{:S(2)}, u32[]{:S(2)}) collective-permute-start(bf16[128,2048]{1,0:T(8,128)(2,1)S(1)} %convolution_convert_fusion.1), channel_id=1, source_target_pairs={{0,8},{8,0},{1,9},{9,1},{2,10},{10,2},{3,11},{11,3},{4,12},{12,4},... | collective-permute-start | bytes 1572872 | tf_op jit(solution)/shard_map/ppermute | solution.py:158
  86.7 10.8 %all-to-all-done.1 = bf16[48,32,128]{2,1,0:T(8,128)(2,1)S(1)} async-done(((bf16[48,32,128]{2,1,0:T(8,128)(2,1)}), bf16[48,32,128]{2,1,0:T(8,128)(2,1)S(1)}, u32[]{:S(2)}, u32[]{:S(2)}) %all-to-all-start.1) | async-done | bytes 393248 | tf_op jit(solution)/shard_map/all_to_all | solution.py:147
  97.5 0.0 copy-start.1
  97.5 0.7 copy-done.1
  98.3 2.8 %shard_map.123 = (f32[256,768]{1,0:T(8,128)}, f32[256,768]{1,0:T(8,128)}) custom-call(bf16[6,256,128]{2,1,0:T(8,128)(2,1)} %bitcast.16, f32[256,768]{1,0:T(8,128)} %outer_ref.3, f32[256,768]{1,0:T(8,128)} %momentum_ref.1), custom_call_target="tpu_custom_call" | custom-call | bytes 3538944 | tf_op jit(solution)/shard_map/pallas_call | solution.py:28
  101.1 0.0 copy-done
  101.1 2.7 %fusion.1.own_ref = f32[128,2048]{1,0:T(8,128)} fusion(bf16[128,512]{1,0:T(8,128)(2,1)} %param.10, bf16[1,2048,512]{2,1,0:T(8,128)(2,1)S(1)} %copy-done), kind=kOutput, calls=%fused_computation.3 | convolution fusion | flops 268435456 | bytes 3276800 | tf_op jit(solution)/shard_map/dot_general | solution.py:159
  103.8 0.0 copy-start.2
  103.8 0.0 collective-permute-done.1.other_ref
  103.8 0.8 copy-done.3
  104.6 5.2 %shard_map.119 = bf16[128,4096]{1,0:T(8,128)(2,1)} custom-call(s32[1]{0:T(128)} %bitcast.upper_ref, bf16[128,4096]{1,0:T(8,128)(2,1)} %hidden_ref.3, bf16[128,4096]{1,0:T(8,128)(2,1)} %res_ref.1, f32[1,4096]{1,0:T(1,128)} %scales_ref.3, f32[128,2048]{1,0:T(8,128)} %fusion.1.own_ref, bf16[128,2048]{1,0:T(8,128)(2,1)} %copy-done.3), custom_call_target="tpu_custom_call" | custom-call | bytes 4734980 | tf_op jit(solution)/shard_map/pallas_call | solution.py:28
  109.8 3.9 %reduce-scatter.2.cloned.1.call-done = bf16[256,512]{1,0:T(8,128)(2,1)} async-done(((bf16[2048,512]{1,0:T(8,128)(2,1)}), bf16[256,512]{1,0:T(8,128)(2,1)}) %reduce-scatter.2.cloned.1.call-update) | async-done | bytes 262160 | tf_op jit(solution)/shard_map/reduce_scatter | solution.py:138
  113.7 0.0 copy-done.2
  113.7 1.1 fusion.6
  114.8 1.3 %dynamic-slice_divide_fusion = f32[1,256]{1,0:T(1,128)} fusion(f32[1,256]{1,0:T(1,128)S(1)} %bitcast.20, f32[1,4096]{1,0:T(1,128)} %scales_ref.3, s32[]{:T(128)S(6)} %select_n.3), kind=kLoop, calls=%fused_computation.13 | loop fusion | flops 256 | bytes 3076 | tf_op jit(solution)/shard_map/div | solution.py:169
  (1 shorter events, 0.0 us)
Async XLA Ops:
  7.2 73.6 %all-gather.3.cloned.1.call-start = ((), (), s32[]{:S(2)}) async-start(), calls=%async_computation.4 | async-start | bytes 2359296 | tf_op jit(solution)/shard_map/all_gather | solution.py:123
  7.9 105.8 %reduce-scatter.2.cloned.1.call-start = ((), (), s32[]{:S(2)}) async-start(), calls=%async_computation.3 | async-start | bytes 2359296 | tf_op jit(solution)/shard_map/reduce_scatter | solution.py:138
  11.3 20.1 %collective-permute-start.2 = (bf16[128,2048]{1,0:T(8,128)(2,1)}, bf16[128,2048]{1,0:T(8,128)(2,1)S(1)}, u32[]{:S(2)}, u32[]{:S(2)}) collective-permute-start(bf16[128,2048]{1,0:T(8,128)(2,1)} %get-tuple-element.10), channel_id=1, source_target_pairs={{0,8},{8,0},{1,9},{9,1},{2,10},{10,2},{3,11},{11,3},{4,12},{12,4},... | collective-permute-start | bytes 1572872 | tf_op jit(solution)/shard_map/ppermute | solution.py:131
  14.6 16.8 %collective-permute-start = (bf16[128,512]{1,0:T(8,128)(2,1)}, bf16[128,512]{1,0:T(8,128)(2,1)S(1)}, u32[]{:S(2)}, u32[]{:S(2)}) collective-permute-start(bf16[128,512]{1,0:T(8,128)(2,1)} %param.10), channel_id=1, source_target_pairs={{0,8},{8,0},{1,9},{9,1},{2,10},{10,2},{3,11},{11,3},{4,12},{12,4},... | collective-permute-start | bytes 393224 | tf_op jit(solution)/shard_map/ppermute | solution.py:124
  72.4 25.1 %all-to-all-start.1 = ((bf16[48,32,128]{2,1,0:T(8,128)(2,1)}), bf16[48,32,128]{2,1,0:T(8,128)(2,1)S(1)}, u32[]{:S(2)}, u32[]{:S(2)}) async-start(bf16[48,32,128]{2,1,0:T(8,128)(2,1)} %shard_map.122), calls=%async_computation.2 | async-start | bytes 786432 | tf_op jit(solution)/shard_map/all_to_all | solution.py:147
  80.8 20.2 %copy-start = (bf16[1,2048,512]{2,1,0:T(8,128)(2,1)S(1)}, bf16[1,2048,512]{2,1,0:T(8,128)(2,1)}, u32[]{:S(2)}) copy-start(bf16[1,2048,512]{2,1,0:T(8,128)(2,1)} %all-gather.3.cloned.1.call-done) | copy-start | bytes 6291460
  83.4 20.4 %collective-permute-start.1 = (bf16[128,2048]{1,0:T(8,128)(2,1)S(1)}, bf16[128,2048]{1,0:T(8,128)(2,1)S(1)}, u32[]{:S(2)}, u32[]{:S(2)}) collective-permute-start(bf16[128,2048]{1,0:T(8,128)(2,1)S(1)} %convolution_convert_fusion.1), channel_id=1, source_target_pairs={{0,8},{8,0},{1,9},{9,1},{2,10},{10,2},{3,11},{11,3},{4,12},{12,4},... | collective-permute-start | bytes 1572872 | tf_op jit(solution)/shard_map/ppermute | solution.py:158
  97.5 0.7 copy-start.1
  103.8 9.9 %copy-start.2 = (bf16[1,256,512]{2,1,0:T(8,128)(2,1)S(1)}, bf16[1,256,512]{2,1,0:T(8,128)(2,1)}, u32[]{:S(2)}) copy-start(bf16[1,256,512]{2,1,0:T(8,128)(2,1)} %param.11) | copy-start | bytes 786436
  103.8 0.8 copy-start.3
Sparse Core Ops, SparseCore 0:
  10.3 52.6 all-gather.2
  66.8 46.8 reduce-scatter.1

commit v2 on v1

--- a/solution.py
+++ b/solution.py
@@ -10,6 +10,8 @@
 REPLICA = AXES[:3]
 FSDP = AXES[3:]
 SWAP = [(0, 1), (1, 0)]
+FORWARD = [(at, (at + 1) % 8) for at in range(8)]
+BACKWARD = [(at, (at + 7) % 8) for at in range(8)]
 f32, bf16 = jnp.float32, jnp.bfloat16
 ROWS = 16
 
@@ -113,10 +115,66 @@
     lax.fori_loop(0, tokens // ROWS, step, 0)
 
 
+def term_kernel(place_ref, kept_ref, received_ref, value_ref, partner_ref, *out_refs):
+    rows = out_refs[-1].shape[0]
+    far_up, far_down, up3, down3, up2, down2, up1, down1, own = out_refs
+    middle = far_up.shape[1]
+
+    def term(step):
+        columns = pl.ds(pl.multiple_of(lax.rem(place_ref[0] + step, 8) * rows, rows), rows)
+        across = (((0,), (0,)), ((), ()))
+        return lax.dot_general(
+            kept_ref[:, columns], value_ref[...], across, preferred_element_type=f32
+        ) + lax.dot_general(
+            received_ref[:, columns], partner_ref[...], across, preferred_element_type=f32
+        )
+
+    far = term(4).astype(bf16)
+    far_up[...] = far[:, :middle]
+    far_down[...] = far[:, middle:]
+    for step, target in ((3, up3), (5, down3), (2, up2), (6, down2), (1, up1), (7, down1), (0, own)):
+        target[...] = term(step).astype(target.dtype)
+
+
+def first_add_kernel(up_ref, down_ref, from_left_ref, from_right_ref, up_out, down_out):
+    middle = from_left_ref.shape[1]
+    low, high = slice(0, middle), slice(middle, 2 * middle)
+    up_out[:, low] = (up_ref[:, low].astype(f32) + from_left_ref[...].astype(f32)).astype(bf16)
+    up_out[:, high] = up_ref[:, high]
+    down_out[:, low] = down_ref[:, low]
+    down_out[:, high] = (
+        down_ref[:, high].astype(f32) + from_right_ref[...].astype(f32)
+    ).astype(bf16)
+
+
+def add_kernel(up_ref, down_ref, from_left_ref, from_right_ref, up_out, down_out):
+    up_out[...] = (up_ref[...].astype(f32) + from_left_ref[...].astype(f32)).astype(bf16)
+    down_out[...] = (down_ref[...].astype(f32) + from_right_ref[...].astype(f32)).astype(bf16)
+
+
+def weight_kernel(
+    place_ref, own_ref, from_left_ref, from_right_ref, weight_ref, scales_ref, grad_ref, gain_ref
+):
+    rows = own_ref.shape[0]
+    total = own_ref[...] + from_left_ref[...].astype(f32) + from_right_ref[...].astype(f32)
+    grad_ref[...] = total.astype(bf16)
+    products = weight_ref[...].astype(f32) * total
+    sums = lax.dot_general(
+        jnp.ones((8, products.shape[1]), f32),
+        products,
+        (((1,), (1,)), ((), ())),
+        precision=lax.Precision.HIGHEST,
+        preferred_element_type=f32,
+    )
+    columns = pl.ds(pl.multiple_of(place_ref[0] * rows, rows), rows)
+    gain_ref[...] = sums[:1, :] / scales_ref[:, columns]
+
+
 def body(
     hidden_in, res_grad, value_grad, value_weight, norm_gain, inner_frag, outer_frag, momentum
 ):
     upper = lax.axis_index("x_hi").reshape(1)
+    place = lax.axis_index("y").reshape(1)
     own_weight = value_weight[0]
     tokens, width = hidden_in.shape
     half = width // 2
@@ -129,13 +187,32 @@
         (upper, hidden_in, norm_gain),
     )
     received = lax.ppermute(sent, "x_hi", SWAP)
-    term = lax.dot_general(
-        jnp.concatenate([kept, received], axis=0),
-        jnp.concatenate([value_grad, partner_value], axis=0),
-        (((0,), (0,)), ((), ())),
-        preferred_element_type=f32,
-    ).astype(bf16)
-    weight_grad = lax.psum_scatter(term, "y", scatter_dimension=0, tiled=True)
+    block = own_weight.shape
+    narrow = (block[0], block[1] // 2)
+    far_up, far_down, up3, down3, up2, down2, up1, down1, own_sum = call(
+        term_kernel,
+        (shape(narrow, bf16),) * 2 + (shape(block, bf16),) * 6 + (shape(block, f32),),
+        (place, kept, received, value_grad, partner_value),
+    )
+
+    def hop(up, down):
+        up = lax.ppermute(up, "y", FORWARD)
+        down = lax.ppermute(down, "y", BACKWARD)
+        return up, down
+
+    pair = (shape(block, bf16),) * 2
+    left, right = hop(far_up, far_down)
+    up3, down3 = call(first_add_kernel, pair, (up3, down3, left, right))
+    left, right = hop(up3, down3)
+    up2, down2 = call(add_kernel, pair, (up2, down2, left, right))
+    left, right = hop(up2, down2)
+    up1, down1 = call(add_kernel, pair, (up1, down1, left, right))
+    left, right = hop(up1, down1)
+    weight_grad, gain_grad = call(
+        weight_kernel,
+        (shape(block, bf16), shape((1, block[0]), f32)),
+        (lax.axis_index(FSDP).reshape(1), own_sum, left, right, own_weight, norm_gain),
+    )
 
     rows, columns = outer_frag.shape
     split = (columns // 128, rows, 128)
@@ -163,12 +240,7 @@
         (upper, hidden_in, res_grad, norm_gain, own_grad, other_grad),
     )
 
-    count = own_weight.shape[0]
-    own_scales = lax.dynamic_slice_in_dim(norm_gain[0], lax.axis_index(FSDP) * count, count, 0)
-    gain_grad = (
-        jnp.sum(own_weight.astype(f32) * weight_grad.astype(f32), axis=1) / own_scales
-    )
-    return (hidden_grad, weight_grad[None], gain_grad[None], new_outer, new_momentum)
+    return (hidden_grad, weight_grad[None], gain_grad, new_outer, new_momentum)
 
 
 def solution(mesh):

time: 123 us -> 154 us (1.25)
  the two profiles are of different devices: /device:TPU:6 before, /device:TPU:26 now
where the time goes in v2:
time: 154 us; the launch traced here: 153 us
  starting transfers between devices  65.3 us (42%)
  waiting for transfers between devices  35.1 us (23%)
  Pallas kernels  27.3 us (18%)
  between operations  14.3 us (9%)
  local copies, waits for them, and re-layouts  5.94 us (4%)
  matrix products  4.98 us (3%)
    pallas_call x10, Pallas kernels, call(): pl.pallas_call(kernel, out_shape=out_shape, in_specs=[scalar() if a.dtype...  27.3 us
    all_to_all x1, starting transfers between devices, body(): spread = lax.all_to_all(pseudo_grad, REPLICA, 0, 0)  17 us
    ppermute x4, starting transfers between devices, hop(): up = lax.ppermute(up, 'y', FORWARD)  16.3 us
    ppermute x1, waiting for transfers between devices, body(): partner_value = lax.ppermute(value_grad, 'x_hi', SWAP)  15.8 us
    ppermute x4, starting transfers between devices, hop(): down = lax.ppermute(down, 'y', BACKWARD)  10.3 us
    all_to_all x1, starting transfers between devices, body(): shared = lax.all_to_all(block, REPLICA, 0, 0)  10.2 us
    ppermute x4, waiting for transfers between devices, hop(): down = lax.ppermute(down, 'y', BACKWARD)  8.36 us
    ppermute x4, waiting for transfers between devices, hop(): up = lax.ppermute(up, 'y', FORWARD)  7.67 us
  transfers between devices with their start and end apart: 14, of which 6 were waited for; matrix products, arithmetic and copies ran while one was open for 3% of the time, Pallas kernels for 14%

profile of v2, /device:TPU:26, one launch (start us, length us, event | category | flops | bytes accessed | tf_op | source)
XLA Modules:
  0.0 152.8 jit_solution(4567799056237070925)
XLA Ops:
  7.9 2.2 %shard_map.126 = bf16[6,256,128]{2,1,0:T(8,128)(2,1)} custom-call(f32[256,768]{1,0:T(8,128)} %outer_ref.3, f32[256,768]{1,0:T(8,128)} %bitcast.18), custom_call_target="tpu_custom_call" | custom-call | bytes 1966080 | tf_op jit(solution)/shard_map/pallas_call | solution.py:30
  10.1 17.0 %all-to-all-start = ((bf16[48,32,128]{2,1,0:T(8,128)(2,1)}), bf16[48,32,128]{2,1,0:T(8,128)(2,1)S(1)}, u32[]{:S(2)}, u32[]{:S(2)}) async-start(bf16[48,32,128]{2,1,0:T(8,128)(2,1)} %bitcast.16), calls=%async_computation | async-start | bytes 786432 | tf_op jit(solution)/shard_map/all_to_all | solution.py:222
  27.1 3.4 %shard_map.120 = (bf16[128,2048]{1,0:T(8,128)(2,1)}, bf16[128,2048]{1,0:T(8,128)(2,1)}) custom-call(s32[1]{0:T(128)} %bitcast.upper_ref, bf16[128,4096]{1,0:T(8,128)(2,1)} %hidden_ref.3, f32[1,4096]{1,0:T(1,128)} %scales_ref.5), custom_call_target="tpu_custom_call" | custom-call | bytes 2113540 | tf_op jit(solution)/shard_map/pallas_call | solution.py:30
  30.5 4.0 %collective-permute-start.2 = (bf16[128,2048]{1,0:T(8,128)(2,1)}, bf16[128,2048]{1,0:T(8,128)(2,1)S(1)}, u32[]{:S(2)}, u32[]{:S(2)}) collective-permute-start(bf16[128,2048]{1,0:T(8,128)(2,1)} %get-tuple-element.27), channel_id=1, source_target_pairs={{0,8},{8,0},{1,9},{9,1},{2,10},{10,2},{3,11},{11,3},{4,12},{12,4},... | collective-permute-start | bytes 1572872 | tf_op jit(solution)/shard_map/ppermute | solution.py:189
  34.5 3.3 %collective-permute-start = (bf16[128,512]{1,0:T(8,128)(2,1)S(1)}, bf16[128,512]{1,0:T(8,128)(2,1)S(1)}, u32[]{:S(2)}, u32[]{:S(2)}) collective-permute-start(bf16[128,512]{1,0:T(8,128)(2,1)S(1)} %copy-done.5), channel_id=1, source_target_pairs={{0,8},{8,0},{1,9},{9,1},{2,10},{10,2},{3,11},{11,3},{4,12},{12,4},... | collective-permute-start | bytes 393224 | tf_op jit(solution)/shard_map/ppermute | solution.py:182
  37.9 15.8 %collective-permute-done.partner_ref = bf16[128,512]{1,0:T(8,128)(2,1)S(1)} collective-permute-done((bf16[128,512]{1,0:T(8,128)(2,1)S(1)}, bf16[128,512]{1,0:T(8,128)(2,1)S(1)}, u32[]{:S(2)}, u32[]{:S(2)}) %collective-permute-start) | collective-permute-done | bytes 131104 | tf_op jit(solution)/shard_map/ppermute | solution.py:182
  54.5 3.4 %shard_map.121 = (bf16[256,256]{1,0:T(8,128)(2,1)}, bf16[256,256]{1,0:T(8,128)(2,1)}, bf16[256,512]{1,0:T(8,128)(2,1)}, bf16[256,512]{1,0:T(8,128)(2,1)}, bf16[2...) custom-call(s32[1]{0:T(128)} %bitcast.3.place_ref, ...), custom_call_target="tpu_custom_call" | custom-call | bytes 3670020 | tf_op jit(solution)/shard_map/pallas_call | solution.py:30
  57.9 4.7 %collective-permute-start.3 = (bf16[256,256]{1,0:T(8,128)(2,1)}, bf16[256,256]{1,0:T(8,128)(2,1)S(1)}, u32[]{:S(2)}, u32[]{:S(2)}) collective-permute-start(bf16[256,256]{1,0:T(8,128)(2,1)} %get-tuple-element.35), channel_id=1, source_target_pairs={{0,1},{1,2},{2,3},{3,4},{4,5},{5,6},{6,7},{7,0},{8,9},{9,10},{10,1... | collective-permute-start | bytes 393224 | tf_op jit(solution)/shard_map/ppermute | solution.py:199
  62.6 2.1 %collective-permute-start.4 = (bf16[256,256]{1,0:T(8,128)(2,1)}, bf16[256,256]{1,0:T(8,128)(2,1)S(1)}, u32[]{:S(2)}, u32[]{:S(2)}) collective-permute-start(bf16[256,256]{1,0:T(8,128)(2,1)} %get-tuple-element.36), channel_id=1, source_target_pairs={{0,7},{1,0},{2,1},{3,2},{4,3},{5,4},{6,5},{7,6},{8,15},{9,8},{10,9... | collective-permute-start | bytes 393224 | tf_op jit(solution)/shard_map/ppermute | solution.py:200
  65.4 1.8 %shard_map.127 = bf16[48,32,128]{2,1,0:T(8,128)(2,1)} custom-call(bf16[48,32,128]{2,1,0:T(8,128)(2,1)} %copy-done.1), custom_call_target="tpu_custom_call" | custom-call | bytes 786432 | tf_op jit(solution)/shard_map/pallas_call | solution.py:30
  67.3 10.2 %all-to-all-start.1 = ((bf16[48,32,128]{2,1,0:T(8,128)(2,1)}), bf16[48,32,128]{2,1,0:T(8,128)(2,1)S(1)}, u32[]{:S(2)}, u32[]{:S(2)}) async-start(bf16[48,32,128]{2,1,0:T(8,128)(2,1)} %shard_map.127), calls=%async_computation.1 | async-start | bytes 786432 | tf_op jit(solution)/shard_map/all_to_all | solution.py:224
  78.2 1.9 %shard_map.122 = (bf16[256,512]{1,0:T(8,128)(2,1)}, bf16[256,512]{1,0:T(8,128)(2,1)}) custom-call(bf16[256,512]{1,0:T(8,128)(2,1)} %get-tuple-element.33.up_ref, bf16[256,512]{1,0:T(8,128)(2,1)} %get-tuple-element.34.down_ref, bf16[256,256]{1,0:T(8,128)(2,1)} %copy-done.14, bf16[256,256]{1,0:T(8,128)(2,1)} %copy-done.15), custom_call_target="tpu_custom_call" | custom-call | bytes 1310720 | tf_op jit(solution)/shard_map/pallas_call | solution.py:30
  80.1 5.1 %collective-permute-start.5 = (bf16[256,512]{1,0:T(8,128)(2,1)}, bf16[256,512]{1,0:T(8,128)(2,1)S(1)}, u32[]{:S(2)}, u32[]{:S(2)}) collective-permute-start(bf16[256,512]{1,0:T(8,128)(2,1)} %get-tuple-element.37), channel_id=1, source_target_pairs={{0,1},{1,2},{2,3},{3,4},{4,5},{5,6},{6,7},{7,0},{8,9},{9,10},{10,1... | collective-permute-start | bytes 786440 | tf_op jit(solution)/shard_map/ppermute | solution.py:199
  85.3 1.9 %collective-permute-start.6 = (bf16[256,512]{1,0:T(8,128)(2,1)}, bf16[256,512]{1,0:T(8,128)(2,1)S(1)}, u32[]{:S(2)}, u32[]{:S(2)}) collective-permute-start(bf16[256,512]{1,0:T(8,128)(2,1)} %get-tuple-element.38), channel_id=1, source_target_pairs={{0,7},{1,0},{2,1},{3,2},{4,3},{5,4},{6,5},{7,6},{8,15},{9,8},{10,9... | collective-permute-start | bytes 786440 | tf_op jit(solution)/shard_map/ppermute | solution.py:200
  87.2 4.2 %collective-permute-done.5.from_left_ref = bf16[256,512]{1,0:T(8,128)(2,1)S(1)} collective-permute-done((bf16[256,512]{1,0:T(8,128)(2,1)}, bf16[256,512]{1,0:T(8,128)(2,1)S(1)}, u32[]{:S(2)}, u32[]{:S(2)}) %collective-permute-start.5) | collective-permute-done | bytes 262176 | tf_op jit(solution)/shard_map/ppermute | solution.py:199
  91.4 5.2 %collective-permute-done.6.from_right_ref = bf16[256,512]{1,0:T(8,128)(2,1)S(1)} collective-permute-done((bf16[256,512]{1,0:T(8,128)(2,1)}, bf16[256,512]{1,0:T(8,128)(2,1)S(1)}, u32[]{:S(2)}, u32[]{:S(2)}) %collective-permute-start.6) | collective-permute-done | bytes 262176 | tf_op jit(solution)/shard_map/ppermute | solution.py:200
  97.3 2.0 %shard_map.123 = (bf16[256,512]{1,0:T(8,128)(2,1)}, bf16[256,512]{1,0:T(8,128)(2,1)}) custom-call(bf16[256,512]{1,0:T(8,128)(2,1)} %get-tuple-element.31.up_ref, bf16[256,512]{1,0:T(8,128)(2,1)} %get-tuple-element.32.down_ref, bf16[256,512]{1,0:T(8,128)(2,1)} %copy-done.10, bf16[256,512]{1,0:T(8,128)(2,1)} %copy-done.12), custom_call_target="tpu_custom_call" | custom-call | bytes 1572864 | tf_op jit(solution)/shard_map/pallas_call | solution.py:30
  99.4 1.9 %collective-permute-start.7 = (bf16[256,512]{1,0:T(8,128)(2,1)}, bf16[256,512]{1,0:T(8,128)(2,1)S(1)}, u32[]{:S(2)}, u32[]{:S(2)}) collective-permute-start(bf16[256,512]{1,0:T(8,128)(2,1)} %get-tuple-element.39), channel_id=1, source_target_pairs={{0,1},{1,2},{2,3},{3,4},{4,5},{5,6},{6,7},{7,0},{8,9},{9,10},{10,1... | collective-permute-start | bytes 786440 | tf_op jit(solution)/shard_map/ppermute | solution.py:199
  101.3 3.9 %collective-permute-start.8 = (bf16[256,512]{1,0:T(8,128)(2,1)}, bf16[256,512]{1,0:T(8,128)(2,1)S(1)}, u32[]{:S(2)}, u32[]{:S(2)}) collective-permute-start(bf16[256,512]{1,0:T(8,128)(2,1)} %get-tuple-element.40), channel_id=1, source_target_pairs={{0,7},{1,0},{2,1},{3,2},{4,3},{5,4},{6,5},{7,6},{8,15},{9,8},{10,9... | collective-permute-start | bytes 786440 | tf_op jit(solution)/shard_map/ppermute | solution.py:200
  105.2 3.4 %collective-permute-done.7.from_left_ref = bf16[256,512]{1,0:T(8,128)(2,1)S(1)} collective-permute-done((bf16[256,512]{1,0:T(8,128)(2,1)}, bf16[256,512]{1,0:T(8,128)(2,1)S(1)}, u32[]{:S(2)}, u32[]{:S(2)}) %collective-permute-start.7) | collective-permute-done | bytes 262176 | tf_op jit(solution)/shard_map/ppermute | solution.py:199
  108.7 3.1 %collective-permute-done.8.from_right_ref = bf16[256,512]{1,0:T(8,128)(2,1)S(1)} collective-permute-done((bf16[256,512]{1,0:T(8,128)(2,1)}, bf16[256,512]{1,0:T(8,128)(2,1)S(1)}, u32[]{:S(2)}, u32[]{:S(2)}) %collective-permute-start.8) | collective-permute-done | bytes 262176 | tf_op jit(solution)/shard_map/ppermute | solution.py:200
  112.5 2.0 %shard_map.124 = (bf16[256,512]{1,0:T(8,128)(2,1)}, bf16[256,512]{1,0:T(8,128)(2,1)}) custom-call(bf16[256,512]{1,0:T(8,128)(2,1)} %get-tuple-element.29.up_ref, bf16[256,512]{1,0:T(8,128)(2,1)} %get-tuple-element.30.down_ref, bf16[256,512]{1,0:T(8,128)(2,1)} %copy-done.11, bf16[256,512]{1,0:T(8,128)(2,1)} %copy-done.13), custom_call_target="tpu_custom_call" | custom-call | bytes 1572864 | tf_op jit(solution)/shard_map/pallas_call | solution.py:30
  114.5 2.4 %collective-permute-start.10 = (bf16[256,512]{1,0:T(8,128)(2,1)}, bf16[256,512]{1,0:T(8,128)(2,1)S(1)}, u32[]{:S(2)}, u32[]{:S(2)}) collective-permute-start(bf16[256,512]{1,0:T(8,128)(2,1)} %get-tuple-element.42), channel_id=1, source_target_pairs={{0,7},{1,0},{2,1},{3,2},{4,3},{5,4},{6,5},{7,6},{8,15},{9,8},{10,9... | collective-permute-start | bytes 786440 | tf_op jit(solution)/shard_map/ppermute | solution.py:200
  117.0 4.6 %collective-permute-start.9 = (bf16[256,512]{1,0:T(8,128)(2,1)}, bf16[256,512]{1,0:T(8,128)(2,1)}, u32[]{:S(2)}, u32[]{:S(2)}) collective-permute-start(bf16[256,512]{1,0:T(8,128)(2,1)} %get-tuple-element.41), channel_id=1, source_target_pairs={{0,1},{1,2},{2,3},{3,4},{4,5},{5,6},{6,7},{7,0},{8,9},{9,10},{10,1... | collective-permute-start | bytes 786440 | tf_op jit(solution)/shard_map/ppermute | solution.py:199
  121.6 3.2 %convolution_convert_fusion = bf16[128,2048]{1,0:T(8,128)(2,1)} fusion(bf16[128,512]{1,0:T(8,128)(2,1)S(1)} %copy-done.8, bf16[1,2048,512]{2,1,0:T(8,128)(2,1)} %all-gather.3.cloned.1.call-done), kind=kOutput, calls=%fused_computation | convolution fusion | flops 268697600 | bytes 2752512 | tf_op jit(solution)/shard_map/dot_general | solution.py:232
  124.8 4.1 %collective-permute-start.1 = (bf16[128,2048]{1,0:T(8,128)(2,1)}, bf16[128,2048]{1,0:T(8,128)(2,1)S(1)}, u32[]{:S(2)}, u32[]{:S(2)}) collective-permute-start(bf16[128,2048]{1,0:T(8,128)(2,1)} %convolution_convert_fusion), channel_id=1, source_target_pairs={{0,8},{8,0},{1,9},{9,1},{2,10},{10,2},{3,11},{11,3},{4,12},{12,4},... | collective-permute-start | bytes 1572872 | tf_op jit(solution)/shard_map/ppermute | solution.py:235
  129.6 2.4 %shard_map.125 = (bf16[256,512]{1,0:T(8,128)(2,1)}, f32[1,256]{1,0:T(1,128)}) custom-call(s32[1]{0:T(128)} %bitcast.2.place_ref, f32[256,512]{1,0:T(8,128)} %get-tuple-element.28.own_ref, bf16[256,512]{1,0:T(8,128)(2,1)} %collective-permute-done.9.from_left_ref, bf16[256,512]{1,0:T(8,128)(2,1)} %copy-done.9, bf16[256,512]{1,0:T(8,128)(2,1)} %bitcast.17, ...), custom_call_target="tpu_custom_call" | custom-call | bytes 1590276 | tf_op jit(solution)/shard_map/pallas_call | solution.py:30
  132.8 2.8 %shard_map.128 = (f32[256,768]{1,0:T(8,128)}, f32[256,768]{1,0:T(8,128)}) custom-call(bf16[6,256,128]{2,1,0:T(8,128)(2,1)} %bitcast.15, f32[256,768]{1,0:T(8,128)} %outer_ref.3, f32[256,768]{1,0:T(8,128)} %momentum_ref.1), custom_call_target="tpu_custom_call" | custom-call | bytes 3538944 | tf_op jit(solution)/shard_map/pallas_call | solution.py:30
  135.7 1.8 %fusion.1.own_ref = f32[128,2048]{1,0:T(8,128)} fusion(bf16[128,512]{1,0:T(8,128)(2,1)S(1)} %copy-done.6, bf16[1,2048,512]{2,1,0:T(8,128)(2,1)S(1)} %copy-done), kind=kOutput, calls=%fused_computation.2 | convolution fusion | flops 268435456 | bytes 3276800 | tf_op jit(solution)/shard_map/dot_general | solution.py:236
  137.4 2.5 %collective-permute-done.1.other_ref = bf16[128,2048]{1,0:T(8,128)(2,1)S(1)} collective-permute-done((bf16[128,2048]{1,0:T(8,128)(2,1)}, bf16[128,2048]{1,0:T(8,128)(2,1)S(1)}, u32[]{:S(2)}, u32[]{:S(2)}) %collective-permute-start.1) | collective-permute-done | bytes 524320 | tf_op jit(solution)/shard_map/ppermute | solution.py:235
  140.0 0.8 copy-done.3
  140.8 5.2 %shard_map.119 = bf16[128,4096]{1,0:T(8,128)(2,1)} custom-call(s32[1]{0:T(128)} %bitcast.upper_ref, bf16[128,4096]{1,0:T(8,128)(2,1)} %hidden_ref.3, bf16[128,4096]{1,0:T(8,128)(2,1)} %res_ref.1, f32[1,4096]{1,0:T(1,128)} %scales_ref.5, f32[128,2048]{1,0:T(8,128)} %fusion.1.own_ref, bf16[128,2048]{1,0:T(8,128)(2,1)} %copy-done.3), custom_call_target="tpu_custom_call" | custom-call | bytes 4734980 | tf_op jit(solution)/shard_map/pallas_call | solution.py:30
  (41 shorter events, 5.9 us)
Async XLA Ops:
  7.2 27.4 %copy-start.5 = (bf16[128,512]{1,0:T(8,128)(2,1)S(1)}, bf16[128,512]{1,0:T(8,128)(2,1)}, u32[]{:S(2)}) copy-start(bf16[128,512]{1,0:T(8,128)(2,1)} %value_ref.1) | copy-start | bytes 393220
  7.2 114.4 %all-gather.3.cloned.1.call-start = ((), (), s32[]{:S(2)}) async-start(), calls=%async_computation.2 | async-start | bytes 2359296 | tf_op jit(solution)/shard_map/all_gather | solution.py:181
  10.1 54.6 %all-to-all-start = ((bf16[48,32,128]{2,1,0:T(8,128)(2,1)}), bf16[48,32,128]{2,1,0:T(8,128)(2,1)S(1)}, u32[]{:S(2)}, u32[]{:S(2)}) async-start(bf16[48,32,128]{2,1,0:T(8,128)(2,1)} %bitcast.16), calls=%async_computation | async-start | bytes 786432 | tf_op jit(solution)/shard_map/all_to_all | solution.py:222
  30.5 23.2 %collective-permute-start.2 = (bf16[128,2048]{1,0:T(8,128)(2,1)}, bf16[128,2048]{1,0:T(8,128)(2,1)S(1)}, u32[]{:S(2)}, u32[]{:S(2)}) collective-permute-start(bf16[128,2048]{1,0:T(8,128)(2,1)} %get-tuple-element.27), channel_id=1, source_target_pairs={{0,8},{8,0},{1,9},{9,1},{2,10},{10,2},{3,11},{11,3},{4,12},{12,4},... | collective-permute-start | bytes 1572872 | tf_op jit(solution)/shard_map/ppermute | solution.py:189
  34.5 19.1 %collective-permute-start = (bf16[128,512]{1,0:T(8,128)(2,1)S(1)}, bf16[128,512]{1,0:T(8,128)(2,1)S(1)}, u32[]{:S(2)}, u32[]{:S(2)}) collective-permute-start(bf16[128,512]{1,0:T(8,128)(2,1)S(1)} %copy-done.5), channel_id=1, source_target_pairs={{0,8},{8,0},{1,9},{9,1},{2,10},{10,2},{3,11},{11,3},{4,12},{12,4},... | collective-permute-start | bytes 393224 | tf_op jit(solution)/shard_map/ppermute | solution.py:182
  53.7 0.7 copy-start.7
  53.7 0.8 copy-start.4
  57.9 19.5 %collective-permute-start.3 = (bf16[256,256]{1,0:T(8,128)(2,1)}, bf16[256,256]{1,0:T(8,128)(2,1)S(1)}, u32[]{:S(2)}, u32[]{:S(2)}) collective-permute-start(bf16[256,256]{1,0:T(8,128)(2,1)} %get-tuple-element.35), channel_id=1, source_target_pairs={{0,1},{1,2},{2,3},{3,4},{4,5},{5,6},{6,7},{7,0},{8,9},{9,10},{10,1... | collective-permute-start | bytes 393224 | tf_op jit(solution)/shard_map/ppermute | solution.py:199
  62.6 59.0 %copy-start.8 = (bf16[128,512]{1,0:T(8,128)(2,1)S(1)}, bf16[128,512]{1,0:T(8,128)(2,1)}, u32[]{:S(2)}) copy-start(bf16[128,512]{1,0:T(8,128)(2,1)} %copy-done.7) | copy-start | bytes 393220
  62.6 14.9 %collective-permute-start.4 = (bf16[256,256]{1,0:T(8,128)(2,1)}, bf16[256,256]{1,0:T(8,128)(2,1)S(1)}, u32[]{:S(2)}, u32[]{:S(2)}) collective-permute-start(bf16[256,256]{1,0:T(8,128)(2,1)} %get-tuple-element.36), channel_id=1, source_target_pairs={{0,7},{1,0},{2,1},{3,2},{4,3},{5,4},{6,5},{7,6},{8,15},{9,8},{10,9... | collective-permute-start | bytes 393224 | tf_op jit(solution)/shard_map/ppermute | solution.py:200
  64.7 0.7 copy-start.1
  67.3 64.8 %all-to-all-start.1 = ((bf16[48,32,128]{2,1,0:T(8,128)(2,1)}), bf16[48,32,128]{2,1,0:T(8,128)(2,1)S(1)}, u32[]{:S(2)}, u32[]{:S(2)}) async-start(bf16[48,32,128]{2,1,0:T(8,128)(2,1)} %shard_map.127), calls=%async_computation.1 | async-start | bytes 786432 | tf_op jit(solution)/shard_map/all_to_all | solution.py:224
  77.5 0.7 copy-start.14
  77.5 0.7 copy-start.15
  80.1 11.3 %collective-permute-start.5 = (bf16[256,512]{1,0:T(8,128)(2,1)}, bf16[256,512]{1,0:T(8,128)(2,1)S(1)}, u32[]{:S(2)}, u32[]{:S(2)}) collective-permute-start(bf16[256,512]{1,0:T(8,128)(2,1)} %get-tuple-element.37), channel_id=1, source_target_pairs={{0,1},{1,2},{2,3},{3,4},{4,5},{5,6},{6,7},{7,0},{8,9},{9,10},{10,1... | collective-permute-start | bytes 786440 | tf_op jit(solution)/shard_map/ppermute | solution.py:199
  85.3 11.4 %collective-permute-start.6 = (bf16[256,512]{1,0:T(8,128)(2,1)}, bf16[256,512]{1,0:T(8,128)(2,1)S(1)}, u32[]{:S(2)}, u32[]{:S(2)}) collective-permute-start(bf16[256,512]{1,0:T(8,128)(2,1)} %get-tuple-element.38), channel_id=1, source_target_pairs={{0,7},{1,0},{2,1},{3,2},{4,3},{5,4},{6,5},{7,6},{8,15},{9,8},{10,9... | collective-permute-start | bytes 786440 | tf_op jit(solution)/shard_map/ppermute | solution.py:200
  91.4 5.2 %copy-start.10 = (bf16[256,512]{1,0:T(8,128)(2,1)}, bf16[256,512]{1,0:T(8,128)(2,1)S(1)}, u32[]{:S(2)}) copy-start(bf16[256,512]{1,0:T(8,128)(2,1)S(1)} %collective-permute-done.5.from_left_ref) | copy-start | bytes 786436
  96.6 0.7 copy-start.12
  99.4 9.3 %collective-permute-start.7 = (bf16[256,512]{1,0:T(8,128)(2,1)}, bf16[256,512]{1,0:T(8,128)(2,1)S(1)}, u32[]{:S(2)}, u32[]{:S(2)}) collective-permute-start(bf16[256,512]{1,0:T(8,128)(2,1)} %get-tuple-element.39), channel_id=1, source_target_pairs={{0,1},{1,2},{2,3},{3,4},{4,5},{5,6},{6,7},{7,0},{8,9},{9,10},{10,1... | collective-permute-start | bytes 786440 | tf_op jit(solution)/shard_map/ppermute | solution.py:199
  101.3 10.5 %collective-permute-start.8 = (bf16[256,512]{1,0:T(8,128)(2,1)}, bf16[256,512]{1,0:T(8,128)(2,1)S(1)}, u32[]{:S(2)}, u32[]{:S(2)}) collective-permute-start(bf16[256,512]{1,0:T(8,128)(2,1)} %get-tuple-element.40), channel_id=1, source_target_pairs={{0,7},{1,0},{2,1},{3,2},{4,3},{5,4},{6,5},{7,6},{8,15},{9,8},{10,9... | collective-permute-start | bytes 786440 | tf_op jit(solution)/shard_map/ppermute | solution.py:200
  108.7 3.1 %copy-start.11 = (bf16[256,512]{1,0:T(8,128)(2,1)}, bf16[256,512]{1,0:T(8,128)(2,1)S(1)}, u32[]{:S(2)}) copy-start(bf16[256,512]{1,0:T(8,128)(2,1)S(1)} %collective-permute-done.7.from_left_ref) | copy-start | bytes 786436
  111.8 0.7 copy-start.13
  114.5 14.4 %collective-permute-start.10 = (bf16[256,512]{1,0:T(8,128)(2,1)}, bf16[256,512]{1,0:T(8,128)(2,1)S(1)}, u32[]{:S(2)}, u32[]{:S(2)}) collective-permute-start(bf16[256,512]{1,0:T(8,128)(2,1)} %get-tuple-element.42), channel_id=1, source_target_pairs={{0,7},{1,0},{2,1},{3,2},{4,3},{5,4},{6,5},{7,6},{8,15},{9,8},{10,9... | collective-permute-start | bytes 786440 | tf_op jit(solution)/shard_map/ppermute | solution.py:200
  117.0 12.0 %collective-permute-start.9 = (bf16[256,512]{1,0:T(8,128)(2,1)}, bf16[256,512]{1,0:T(8,128)(2,1)}, u32[]{:S(2)}, u32[]{:S(2)}) collective-permute-start(bf16[256,512]{1,0:T(8,128)(2,1)} %get-tuple-element.41), channel_id=1, source_target_pairs={{0,1},{1,2},{2,3},{3,4},{4,5},{5,6},{6,7},{7,0},{8,9},{9,10},{10,1... | collective-permute-start | bytes 786440 | tf_op jit(solution)/shard_map/ppermute | solution.py:199
  124.8 10.8 %copy-start = (bf16[1,2048,512]{2,1,0:T(8,128)(2,1)S(1)}, bf16[1,2048,512]{2,1,0:T(8,128)(2,1)}, u32[]{:S(2)}) copy-start(bf16[1,2048,512]{2,1,0:T(8,128)(2,1)} %all-gather.3.cloned.1.call-done) | copy-start | bytes 6291460
  124.8 10.8 %copy-start.6 = (bf16[128,512]{1,0:T(8,128)(2,1)S(1)}, bf16[128,512]{1,0:T(8,128)(2,1)}, u32[]{:S(2)}) copy-start(bf16[128,512]{1,0:T(8,128)(2,1)} %value_ref.1) | copy-start | bytes 393220
  124.8 15.1 %collective-permute-start.1 = (bf16[128,2048]{1,0:T(8,128)(2,1)}, bf16[128,2048]{1,0:T(8,128)(2,1)S(1)}, u32[]{:S(2)}, u32[]{:S(2)}) collective-permute-start(bf16[128,2048]{1,0:T(8,128)(2,1)} %convolution_convert_fusion), channel_id=1, source_target_pairs={{0,8},{8,0},{1,9},{9,1},{2,10},{10,2},{3,11},{11,3},{4,12},{12,4},... | collective-permute-start | bytes 1572872 | tf_op jit(solution)/shard_map/ppermute | solution.py:235
  128.9 0.7 copy-start.9
  132.1 0.8 copy-start.2
  140.0 0.8 copy-start.3
Sparse Core Ops, SparseCore 0:
  10.4 52.0 all-gather.2

commit v3 on v1

v3 whole, which is shorter than its diff:
```python
import jax
import jax.numpy as jnp
from jax import lax
from jax.experimental import pallas as pl
from jax.experimental.pallas import tpu as pltpu
from jax.sharding import Mesh, PartitionSpec as P


AXES = ("x_lo", "z", "core", "x_hi", "y")
REPLICA = AXES[:3]
FSDP = AXES[3:]
SWAP = [(0, 1), (1, 0)]
f32, bf16 = jnp.float32, jnp.bfloat16
ROWS = 16


def whole():
    return pl.BlockSpec(memory_space=pltpu.VMEM)


def scalar():
    return pl.BlockSpec(memory_space=pltpu.SMEM)


def call(kernel, out_shape, operands, flops=0):
    outs = out_shape if isinstance(out_shape, (tuple, list)) else (out_shape,)
    moved = sum(a.size * a.dtype.itemsize for a in (*operands, *outs))
    return pl.pallas_call(
        kernel,
        out_shape=out_shape,
        in_specs=[scalar() if a.dtype == jnp.int32 else whole() for a in operands],
        out_specs=jax.tree.map(lambda _: whole(), out_shape),
        cost_estimate=pl.CostEstimate(flops=flops, bytes_accessed=moved, transcendentals=0),
    )(*operands)


def shape(dims, dtype):
    return jax.ShapeDtypeStruct(dims, dtype)


def inverse_of(rows):
    return lax.rsqrt(jnp.mean(rows * rows, axis=1, keepdims=True) + 1e-05)


def norm_kernel(hidden_ref, scales_ref, out_ref):
    peers, tokens, width = out_ref.shape
    half, piece = peers * width // 2, width // 2

    def step(index, _):
        at = pl.ds(pl.multiple_of(index * ROWS, ROWS), ROWS)
        inverse = inverse_of(hidden_ref[at, :].astype(f32))
        for peer in range(peers):
            for side in range(2):
                columns = pl.ds(side * half + peer * piece, piece)
                unit = hidden_ref[at, columns].astype(f32) * inverse
                normed = (unit * scales_ref[:, columns]).astype(bf16)
                out_ref[peer, at, pl.ds(side * piece, piece)] = normed
        return 0

    lax.fori_loop(0, tokens // ROWS, step, 0)


def grad_kernel(upper_ref, value_ref, own_ref, other_ref, out_ref):
    piece = own_ref.shape[0]
    for side, weight_ref in ((upper_ref[0], own_ref), (1 - upper_ref[0], other_ref)):
        columns = pl.ds(pl.multiple_of(side * piece, piece), piece)
        weight = weight_ref[...]
        for peer in range(value_ref.shape[0]):
            grad = lax.dot_general(
                value_ref[peer], weight, (((1,), (1,)), ((), ())), preferred_element_type=f32
            )
            out_ref[peer, :, columns] = grad.astype(bf16)


def weight_kernel(upper_ref, normed_ref, value_ref, own_ref, sent_ref):
    piece = own_ref.shape[0]
    for side, target in ((1 - upper_ref[0], sent_ref), (upper_ref[0], own_ref)):
        columns = pl.ds(pl.multiple_of(side * piece, piece), piece)
        target[...] = lax.dot_general(
            normed_ref[:, columns],
            value_ref[...],
            (((0,), (0,)), ((), ())),
            preferred_element_type=f32,
        ).astype(target.dtype)


def quarter(place_ref, step, rows):
    core = lax.rem(place_ref[0] + step // 2, 2)
    side = lax.rem(place_ref[1] + step % 2, 2)
    return pl.ds(pl.multiple_of((core * 2 + side) * rows, rows), rows)


def pseudo_kernel(place_ref, outer_ref, inner_ref, own_ref, *sent_refs):
    rows = own_ref.shape[0]
    for step, target in enumerate((own_ref, *sent_refs)):
        at = quarter(place_ref, step, rows)
        target[...] = (outer_ref[at, :] - inner_ref[at, :]).astype(target.dtype)


def fold_kernel(own_ref, first_ref, second_ref, third_ref, out_ref):
    total = own_ref[...]
    for ref in (first_ref, second_ref, third_ref):
        total += ref[...].astype(f32)
    out_ref[...] = total.astype(bf16)


def mean_kernel(sums_ref, out_ref):
    def step(index, _):
        at = pl.ds(pl.multiple_of(index * ROWS, ROWS), ROWS)
        total = sums_ref[0, at, :].astype(f32)
        for part in range(1, sums_ref.shape[0]):
            total += sums_ref[part, at, :].astype(f32)
        out_ref[at, :] = (total / 48).astype(bf16)
        return 0

    lax.fori_loop(0, out_ref.shape[0] // ROWS, step, 0)


def outer_kernel(
    place_ref,
    own_ref,
    first_ref,
    second_ref,
    third_ref,
    outer_ref,
    momentum_ref,
    new_outer_ref,
    new_momentum_ref,
):
    for step, ref in enumerate((own_ref, first_ref, second_ref, third_ref)):
        at = quarter(place_ref, step, own_ref.shape[0])
        average = ref[...].astype(f32)
        new_momentum = 0.9 * momentum_ref[at, :] + average
        new_momentum_ref[at, :] = new_momentum
        new_outer_ref[at, :] = outer_ref[at, :] - 0.7 * (average + 0.9 * new_momentum)


def total_kernel(
    place_ref, own_ref, received_ref, weight_ref, scales_ref, grad_ref, gain_ref
):
    rows = own_ref.shape[0]
    total = own_ref[...] + received_ref[...].astype(f32)
    grad_ref[...] = total.astype(bf16)
    products = weight_ref[...].astype(f32) * total
    sums = lax.dot_general(
        jnp.ones((8, products.shape[1]), f32),
        products,
        (((1,), (1,)), ((), ())),
        precision=lax.Precision.HIGHEST,
        preferred_element_type=f32,
    )
    columns = pl.ds(pl.multiple_of(place_ref[0] * rows, rows), rows)
    gain_ref[...] = sums[:1, :] / scales_ref[:, columns]


def hidden_kernel(hidden_ref, res_ref, scales_ref, grad_ref, out_ref):
    peers, tokens, width = grad_ref.shape
    half, piece = peers * width // 2, width // 2

    def step(index, _):
        at = pl.ds(pl.multiple_of(index * ROWS, ROWS), ROWS)
        inverse = inverse_of(hidden_ref[at, :].astype(f32))

        def pieces():
            for peer in range(peers):
                for side in range(2):
                    columns = pl.ds(side * half + peer * piece, piece)
                    grad = grad_ref[peer, at, pl.ds(side * piece, piece)].astype(f32)
                    scaled = grad * scales_ref[:, columns]
                    yield columns, scaled, hidden_ref[at, columns].astype(f32) * inverse

        total = jnp.zeros((ROWS, piece), f32)
        for _, scaled, unit in pieces():
            total += scaled * unit
        projection = jnp.sum(total, axis=1, keepdims=True) / (2 * half)
        for columns, scaled, unit in pieces():
            grad = res_ref[at, columns].astype(f32) + inverse * (scaled - unit * projection)
            out_ref[at, columns] = grad.astype(bf16)
        return 0

    lax.fori_loop(0, tokens // ROWS, step, 0)


def body(
    hidden_in, res_grad, value_grad, value_weight, norm_gain, inner_frag, outer_frag, momentum
):
    upper = lax.axis_index("x_hi").reshape(1)
    own_weight = value_weight[0]
    tokens, width = hidden_in.shape
    count, features = own_weight.shape
    peers = lax.axis_size("y")
    values = lax.all_gather(value_grad, "y", axis=0)
    other_weight = lax.ppermute(own_weight, "x_hi", SWAP)

    exchange = shape((peers, tokens, width // peers), bf16)
    normed = call(norm_kernel, exchange, (hidden_in, norm_gain))
    normed = lax.all_to_all(normed, "y", 0, 0)
    grads = call(grad_kernel, exchange, (upper, values, own_weight, other_weight))
    grads = lax.all_to_all(grads, "y", 0, 0)
    own_sum, sent_sum = call(
        weight_kernel,
        (shape((count, features), f32), shape((count, features), bf16)),
        (
            upper,
            normed.reshape(peers * tokens, -1),
            values.reshape(peers * tokens, features),
        ),
    )
    received = lax.ppermute(sent_sum, "x_hi", SWAP)

    rows, columns = outer_frag.shape
    piece = (rows // 4, columns)
    place = jnp.stack([lax.axis_index("core"), lax.axis_index("x_lo")])

    def trade(parts):
        received = []
        for step, part in zip((1, 2, 3), parts):
            table = [(at, at ^ (step // 2 + step % 2 * 2)) for at in range(4)]
            received.append(lax.ppermute(part, ("x_lo", "core"), table))
        return received

    own_part, *sent_parts = call(
        pseudo_kernel,
        (shape(piece, f32),) + (shape(piece, bf16),) * 3,
        (place, outer_frag, inner_frag[0]),
    )
    received_parts = trade(sent_parts)
    part = call(fold_kernel, shape(piece, bf16), (own_part, *received_parts))
    parts = lax.all_gather(part, "z", axis=0)
    mean = call(mean_kernel, shape(piece, bf16), (parts,))
    means = trade((mean,) * 3)
    new_outer, new_momentum = call(
        outer_kernel,
        (shape(outer_frag.shape, f32), shape(outer_frag.shape, f32)),
        (place, mean, *means, outer_frag, momentum),
    )
    weight_grad, gain_grad = call(
        total_kernel,
        (shape((count, features), bf16), shape((1, count), f32)),
        (lax.axis_index(FSDP).reshape(1), own_sum, received, own_weight, norm_gain),
    )

    hidden_grad = call(
        hidden_kernel, shape(hidden_in.shape, bf16), (hidden_in, res_grad, norm_gain, grads)
    )
    return (hidden_grad, weight_grad[None], gain_grad, new_outer, new_momentum)


def solution(mesh):
    grid = Mesh(mesh.devices.reshape(2, 12, 2, 2, 8), AXES)
    in_specs = (
        P(AXES, None),
        P(AXES, None),
        P(AXES, None),
        P(REPLICA, FSDP, None),
        P(REPLICA, None),
        P(REPLICA, FSDP, None),
        P(FSDP, None),
        P(FSDP, None),
    )
    out_specs = (
        P(AXES, None),
        P(REPLICA, FSDP, None),
        P(REPLICA, FSDP),
        P(FSDP, None),
        P(FSDP, None),
    )

    def step(*arrays):
        return body(*arrays)

    step = jax.shard_map(step, mesh=grid, in_specs=in_specs, out_specs=out_specs, check_vma=False)
    return step
```

time: 123 us -> 159 us (1.29)
  the two profiles are of different devices: /device:TPU:6 before, /device:TPU:1 now
where the time goes in v3:
time: 159 us
  waiting for transfers between devices  67.4 us (42%)
  starting transfers between devices  46.8 us (29%)
  Pallas kernels  26.5 us (17%)
  between operations  14.2 us (9%)
  local copies, waits for them, and re-layouts  2.97 us (2%)
    all_gather x1, waiting for transfers between devices, body(): parts = lax.all_gather(part, 'z', axis=0)  43.5 us
    ppermute x6, starting transfers between devices, trade(): received.append(lax.ppermute(part, ('x_lo', 'core'), table))  28.9 us
    pallas_call x9, Pallas kernels, call(): pl.pallas_call(kernel, out_shape=out_shape, in_specs=[scalar() if a.dtype...  26.5 us
    ppermute x1, waiting for transfers between devices, body(): other_weight = lax.ppermute(own_weight, 'x_hi', SWAP)  9.34 us
    all_gather x1, waiting for transfers between devices, body(): values = lax.all_gather(value_grad, 'y', axis=0)  8.86 us
    all_to_all x1, starting transfers between devices, body(): normed = lax.all_to_all(normed, 'y', 0, 0)  7.64 us
    ppermute x6, waiting for transfers between devices, trade(): received.append(lax.ppermute(part, ('x_lo', 'core'), table))  5.01 us
    ppermute x1, starting transfers between devices, body(): received = lax.ppermute(sent_sum, 'x_hi', SWAP)  4.56 us
  transfers between devices with their start and end apart: 12, of which 5 were waited for; matrix products, arithmetic and copies ran while one was open for 0% of the time, Pallas kernels for 14%

profile of v3, /device:TPU:1, one launch (start us, length us, event | category | flops | bytes accessed | tf_op | source)
XLA Modules:
  0.0 158.5 jit_solution(7809292199504941715)
XLA Ops:
  7.2 0.0 all-gather.5.cloned.1.call-start
  7.2 0.7 all-gather.5.cloned.1.call-update
  7.9 3.3 %shard_map.121 = bf16[8,128,512]{2,1,0:T(8,128)(2,1)} custom-call(bf16[128,4096]{1,0:T(8,128)(2,1)} %hidden_ref.3, f32[1,4096]{1,0:T(1,128)} %scales_ref.5), custom_call_target="tpu_custom_call" | custom-call | bytes 2113536 | tf_op jit(solution)/shard_map/pallas_call | solution.py:28
  11.2 7.6 %all-to-all-start.1 = ((bf16[8,128,512]{2,1,0:T(8,128)(2,1)}), bf16[8,128,512]{2,1,0:T(8,128)(2,1)S(1)}, u32[]{:S(2)}, u32[]{:S(2)}) async-start(bf16[8,128,512]{2,1,0:T(8,128)(2,1)} %shard_map.121), calls=%async_computation.1 | async-start | bytes 2097152 | tf_op jit(solution)/shard_map/all_to_all | solution.py:197
  18.9 0.0 all-gather.7.cloned.1.call-start
  18.9 0.7 pad_add_fusion.place_ref
  19.6 2.2 %shard_map.124 = (f32[64,768]{1,0:T(8,128)}, bf16[64,768]{1,0:T(8,128)(2,1)}, bf16[64,768]{1,0:T(8,128)(2,1)}, bf16[64,768]{1,0:T(8,128)(2,1)}) custom-call(s32[2]{0:T(128)} %pad_add_fusion.place_ref, f32[256,768]{1,0:T(8,128)} %outer_ref.3, f32[256,768]{1,0:T(8,128)} %bitcast.16), custom_call_target="tpu_custom_call" | custom-call | bytes 2064392 | tf_op jit(solution)/shard_map/pallas_call | solution.py:28
  21.8 3.1 %collective-permute-start.2 = (bf16[64,768]{1,0:T(8,128)(2,1)}, bf16[64,768]{1,0:T(8,128)(2,1)S(1)}, u32[]{:S(2)}, u32[]{:S(2)}) collective-permute-start(bf16[64,768]{1,0:T(8,128)(2,1)} %get-tuple-element.20), channel_id=1, source_target_pairs={{0,384},{16,400},{384,0},{400,16},{1,385},{17,401},{385,1},{401,17... | collective-permute-start | bytes 294920 | tf_op jit(solution)/shard_map/ppermute | solution.py:219
  24.9 7.1 %collective-permute-start.3 = (bf16[64,768]{1,0:T(8,128)(2,1)}, bf16[64,768]{1,0:T(8,128)(2,1)S(1)}, u32[]{:S(2)}, u32[]{:S(2)}) collective-permute-start(bf16[64,768]{1,0:T(8,128)(2,1)} %get-tuple-element.21), channel_id=1, source_target_pairs={{0,16},{16,0},{384,400},{400,384},{1,17},{17,1},{385,401},{401,385... | collective-permute-start | bytes 294920 | tf_op jit(solution)/shard_map/ppermute | solution.py:219
  32.1 3.5 %collective-permute-start.4 = (bf16[64,768]{1,0:T(8,128)(2,1)}, bf16[64,768]{1,0:T(8,128)(2,1)S(1)}, u32[]{:S(2)}, u32[]{:S(2)}) collective-permute-start(bf16[64,768]{1,0:T(8,128)(2,1)} %get-tuple-element.22), channel_id=1, source_target_pairs={{0,400},{16,384},{384,16},{400,0},{1,401},{17,385},{385,17},{401,1... | collective-permute-start | bytes 294920 | tf_op jit(solution)/shard_map/ppermute | solution.py:219
  35.7 3.7 %collective-permute-done.4.third_ref = bf16[64,768]{1,0:T(8,128)(2,1)S(1)} collective-permute-done((bf16[64,768]{1,0:T(8,128)(2,1)}, bf16[64,768]{1,0:T(8,128)(2,1)S(1)}, u32[]{:S(2)}, u32[]{:S(2)}) %collective-permute-start.4) | collective-permute-done | bytes 98336 | tf_op jit(solution)/shard_map/ppermute | solution.py:219
  39.4 0.6 copy-done.10
  40.0 1.8 %shard_map.125 = bf16[64,768]{1,0:T(8,128)(2,1)} custom-call(f32[64,768]{1,0:T(8,128)} %get-tuple-element.19.own_ref, bf16[64,768]{1,0:T(8,128)(2,1)} %copy-done.8, bf16[64,768]{1,0:T(8,128)(2,1)} %copy-done.9, bf16[64,768]{1,0:T(8,128)(2,1)} %copy-done.10), custom_call_target="tpu_custom_call" | custom-call | bytes 589824 | tf_op jit(solution)/shard_map/pallas_call | solution.py:28
  41.8 1.9 %collective-permute-start = (bf16[256,512]{1,0:T(8,128)(2,1)S(1)}, bf16[256,512]{1,0:T(8,128)(2,1)S(1)}, u32[]{:S(2)}, u32[]{:S(2)}) collective-permute-start(bf16[256,512]{1,0:T(8,128)(2,1)S(1)} %bitcast.15), channel_id=1, source_target_pairs={{0,8},{8,0},{1,9},{9,1},{2,10},{10,2},{3,11},{11,3},{4,12},{12,4},... | collective-permute-start | bytes 786440 | tf_op jit(solution)/shard_map/ppermute | solution.py:193
  43.7 9.3 %collective-permute-done.other_ref = bf16[256,512]{1,0:T(8,128)(2,1)S(1)} collective-permute-done((bf16[256,512]{1,0:T(8,128)(2,1)S(1)}, bf16[256,512]{1,0:T(8,128)(2,1)S(1)}, u32[]{:S(2)}, u32[]{:S(2)}) %collective-permute-start) | collective-permute-done | bytes 262176 | tf_op jit(solution)/shard_map/ppermute | solution.py:193
  53.1 8.9 %all-gather.5.cloned.1.call-done.value_ref = bf16[1024,512]{1,0:T(8,128)(2,1)} async-done(((bf16[128,512]{1,0:T(8,128)(2,1)}), bf16[1024,512]{1,0:T(8,128)(2,1)}) %all-gather.5.cloned.1.call-update) | async-done | bytes 1048592 | tf_op jit(solution)/shard_map/all_gather | solution.py:192
  62.0 3.8 %shard_map.119 = bf16[8,128,512]{2,1,0:T(8,128)(2,1)} custom-call(s32[1]{0:T(128)} %bitcast.upper_ref, bf16[8,128,512]{2,1,0:T(8,128)(2,1)} %bitcast.10, bf16[256,512]{1,0:T(8,128)(2,1)} %bitcast.13, bf16[256,512]{1,0:T(8,128)(2,1)} %copy-done.4), custom_call_target="tpu_custom_call" | custom-call | bytes 2621444 | tf_op jit(solution)/shard_map/pallas_call | solution.py:28
  65.7 3.8 %all-to-all-start = ((bf16[8,128,512]{2,1,0:T(8,128)(2,1)}), bf16[8,128,512]{2,1,0:T(8,128)(2,1)S(1)}, u32[]{:S(2)}, u32[]{:S(2)}) async-start(bf16[8,128,512]{2,1,0:T(8,128)(2,1)} %shard_map.119), calls=%async_computation | async-start | bytes 2097152 | tf_op jit(solution)/shard_map/all_to_all | solution.py:199
  69.5 3.1 %shard_map.122 = (f32[256,512]{1,0:T(8,128)}, bf16[256,512]{1,0:T(8,128)(2,1)}) custom-call(s32[1]{0:T(128)} %bitcast.upper_ref, bf16[1024,512]{1,0:T(8,128)(2,1)} %bitcast.11, bf16[1024,512]{1,0:T(8,128)(2,1)} %all-gather.5.cloned.1.call-done.value_ref), custom_call_target="tpu_custom_call" | custom-call | bytes 2883588 | tf_op jit(solution)/shard_map/pallas_call | solution.py:28
  72.6 4.6 %collective-permute-start.1 = (bf16[256,512]{1,0:T(8,128)(2,1)}, bf16[256,512]{1,0:T(8,128)(2,1)S(1)}, u32[]{:S(2)}, u32[]{:S(2)}) collective-permute-start(bf16[256,512]{1,0:T(8,128)(2,1)} %get-tuple-element.16), channel_id=1, source_target_pairs={{0,8},{8,0},{1,9},{9,1},{2,10},{10,2},{3,11},{11,3},{4,12},{12,4},... | collective-permute-start | bytes 786440 | tf_op jit(solution)/shard_map/ppermute | solution.py:209
  77.1 43.5 %all-gather.7.cloned.1.call-done = bf16[768,768]{1,0:T(8,128)(2,1)} async-done(((bf16[64,768]{1,0:T(8,128)(2,1)}), bf16[768,768]{1,0:T(8,128)(2,1)}) %all-gather.7.cloned.1.call-update) | async-done | bytes 1179664 | tf_op jit(solution)/shard_map/all_gather | solution.py:229
  120.6 2.1 %shard_map.126.own_ref = bf16[64,768]{1,0:T(8,128)(2,1)} custom-call(bf16[12,64,768]{2,1,0:T(8,128)(2,1)} %bitcast.12), custom_call_target="tpu_custom_call" | custom-call | bytes 1277952 | tf_op jit(solution)/shard_map/pallas_call | solution.py:28
  122.7 3.0 %collective-permute-start.5 = (bf16[64,768]{1,0:T(8,128)(2,1)}, bf16[64,768]{1,0:T(8,128)(2,1)S(1)}, u32[]{:S(2)}, u32[]{:S(2)}) collective-permute-start(bf16[64,768]{1,0:T(8,128)(2,1)} %shard_map.126.own_ref), channel_id=1, source_target_pairs={{0,384},{16,400},{384,0},{400,16},{1,385},{17,401},{385,1},{401,17... | collective-permute-start | bytes 294920 | tf_op jit(solution)/shard_map/ppermute | solution.py:219
  125.7 9.9 %collective-permute-start.6 = (bf16[64,768]{1,0:T(8,128)(2,1)}, bf16[64,768]{1,0:T(8,128)(2,1)S(1)}, u32[]{:S(2)}, u32[]{:S(2)}) collective-permute-start(bf16[64,768]{1,0:T(8,128)(2,1)} %shard_map.126.own_ref), channel_id=1, source_target_pairs={{0,16},{16,0},{384,400},{400,384},{1,17},{17,1},{385,401},{401,385... | collective-permute-start | bytes 294920 | tf_op jit(solution)/shard_map/ppermute | solution.py:219
  135.7 2.2 %collective-permute-start.7 = (bf16[64,768]{1,0:T(8,128)(2,1)}, bf16[64,768]{1,0:T(8,128)(2,1)S(1)}, u32[]{:S(2)}, u32[]{:S(2)}) collective-permute-start(bf16[64,768]{1,0:T(8,128)(2,1)} %shard_map.126.own_ref), channel_id=1, source_target_pairs={{0,400},{16,384},{384,16},{400,0},{1,401},{17,385},{385,17},{401,1... | collective-permute-start | bytes 294920 | tf_op jit(solution)/shard_map/ppermute | solution.py:219
  137.9 0.7 copy-done.3
  138.6 2.3 %shard_map.123 = (bf16[256,512]{1,0:T(8,128)(2,1)}, f32[1,256]{1,0:T(1,128)}) custom-call(s32[1]{0:T(128)} %bitcast.3.place_ref, f32[256,512]{1,0:T(8,128)} %get-tuple-element.15.own_ref, bf16[256,512]{1,0:T(8,128)(2,1)} %copy-done.3, bf16[256,512]{1,0:T(8,128)(2,1)} %bitcast.14, f32[1,4096]{1,0:T(1,128)} %scales_ref.5), custom_call_target="tpu_custom_call" | custom-call | bytes 1328132 | tf_op jit(solution)/shard_map/pallas_call | solution.py:28
  140.9 1.3 collective-permute-done.7.third_ref
  142.2 0.6 copy-done.7
  142.8 2.9 %shard_map.127 = (f32[256,768]{1,0:T(8,128)}, f32[256,768]{1,0:T(8,128)}) custom-call(s32[2]{0:T(128)} %pad_add_fusion.place_ref, bf16[64,768]{1,0:T(8,128)(2,1)} %shard_map.126.own_ref, bf16[64,768]{1,0:T(8,128)(2,1)} %copy-done.5, bf16[64,768]{1,0:T(8,128)(2,1)} %copy-done.6, bf16[64,768]{1,0:T(8,128)(2,1)} %copy-done.7, f32[256,768]{1,0:T(8,128)} %outer_ref.3, ...), custom_call_target="tpu_custom_call" | custom-call | bytes 3538952 | tf_op jit(solution)/shard_map/pallas_call | solution.py:28
  145.8 1.0 copy-done.1
  146.7 4.9 %shard_map.120 = bf16[128,4096]{1,0:T(8,128)(2,1)} custom-call(bf16[128,4096]{1,0:T(8,128)(2,1)} %hidden_ref.3, bf16[128,4096]{1,0:T(8,128)(2,1)} %res_ref.1, f32[1,4096]{1,0:T(1,128)} %scales_ref.5, bf16[8,128,512]{2,1,0:T(8,128)(2,1)} %copy-done.1), custom_call_target="tpu_custom_call" | custom-call | bytes 4210688 | tf_op jit(solution)/shard_map/pallas_call | solution.py:28
  (26 shorter events, 0.1 us)
Async XLA Ops:
  7.2 54.8 %all-gather.5.cloned.1.call-start = ((), (), s32[]{:S(2)}) async-start(), calls=%async_computation.2 | async-start | bytes 1179648 | tf_op jit(solution)/shard_map/all_gather | solution.py:192
  11.2 54.5 %all-to-all-start.1 = ((bf16[8,128,512]{2,1,0:T(8,128)(2,1)}), bf16[8,128,512]{2,1,0:T(8,128)(2,1)S(1)}, u32[]{:S(2)}, u32[]{:S(2)}) async-start(bf16[8,128,512]{2,1,0:T(8,128)(2,1)} %shard_map.121), calls=%async_computation.1 | async-start | bytes 2097152 | tf_op jit(solution)/shard_map/all_to_all | solution.py:197
  18.9 22.9 %copy-start.2 = (bf16[1,256,512]{2,1,0:T(8,128)(2,1)S(1)}, bf16[1,256,512]{2,1,0:T(8,128)(2,1)}, u32[]{:S(2)}) copy-start(bf16[1,256,512]{2,1,0:T(8,128)(2,1)} %param.11) | copy-start | bytes 786436
  18.9 101.7 %all-gather.7.cloned.1.call-start = ((), (), s32[]{:S(2)}) async-start(), calls=%async_computation.3 | async-start | bytes 1277952 | tf_op jit(solution)/shard_map/all_gather | solution.py:229
  21.8 13.8 %collective-permute-start.2 = (bf16[64,768]{1,0:T(8,128)(2,1)}, bf16[64,768]{1,0:T(8,128)(2,1)S(1)}, u32[]{:S(2)}, u32[]{:S(2)}) collective-permute-start(bf16[64,768]{1,0:T(8,128)(2,1)} %get-tuple-element.20), channel_id=1, source_target_pairs={{0,384},{16,400},{384,0},{400,16},{1,385},{17,401},{385,1},{401,17... | collective-permute-start | bytes 294920 | tf_op jit(solution)/shard_map/ppermute | solution.py:219
  24.9 10.7 %collective-permute-start.3 = (bf16[64,768]{1,0:T(8,128)(2,1)}, bf16[64,768]{1,0:T(8,128)(2,1)S(1)}, u32[]{:S(2)}, u32[]{:S(2)}) collective-permute-start(bf16[64,768]{1,0:T(8,128)(2,1)} %get-tuple-element.21), channel_id=1, source_target_pairs={{0,16},{16,0},{384,400},{400,384},{1,17},{17,1},{385,401},{401,385... | collective-permute-start | bytes 294920 | tf_op jit(solution)/shard_map/ppermute | solution.py:219
  32.1 7.3 %collective-permute-start.4 = (bf16[64,768]{1,0:T(8,128)(2,1)}, bf16[64,768]{1,0:T(8,128)(2,1)S(1)}, u32[]{:S(2)}, u32[]{:S(2)}) collective-permute-start(bf16[64,768]{1,0:T(8,128)(2,1)} %get-tuple-element.22), channel_id=1, source_target_pairs={{0,400},{16,384},{384,16},{400,0},{1,401},{17,385},{385,17},{401,1... | collective-permute-start | bytes 294920 | tf_op jit(solution)/shard_map/ppermute | solution.py:219
  35.6 3.8 %copy-start.8 = (bf16[64,768]{1,0:T(8,128)(2,1)}, bf16[64,768]{1,0:T(8,128)(2,1)S(1)}, u32[]{:S(2)}) copy-start(bf16[64,768]{1,0:T(8,128)(2,1)S(1)} %collective-permute-done.2.first_ref) | copy-start | bytes 294916
  35.7 3.7 %copy-start.9 = (bf16[64,768]{1,0:T(8,128)(2,1)}, bf16[64,768]{1,0:T(8,128)(2,1)S(1)}, u32[]{:S(2)}) copy-start(bf16[64,768]{1,0:T(8,128)(2,1)S(1)} %collective-permute-done.3.second_ref) | copy-start | bytes 294916
  39.4 0.6 copy-start.10
  41.8 11.3 %collective-permute-start = (bf16[256,512]{1,0:T(8,128)(2,1)S(1)}, bf16[256,512]{1,0:T(8,128)(2,1)S(1)}, u32[]{:S(2)}, u32[]{:S(2)}) collective-permute-start(bf16[256,512]{1,0:T(8,128)(2,1)S(1)} %bitcast.15), channel_id=1, source_target_pairs={{0,8},{8,0},{1,9},{9,1},{2,10},{10,2},{3,11},{11,3},{4,12},{12,4},... | collective-permute-start | bytes 786440 | tf_op jit(solution)/shard_map/ppermute | solution.py:193
  53.1 8.9 %copy-start.4 = (bf16[256,512]{1,0:T(8,128)(2,1)}, bf16[256,512]{1,0:T(8,128)(2,1)S(1)}, u32[]{:S(2)}) copy-start(bf16[256,512]{1,0:T(8,128)(2,1)S(1)} %collective-permute-done.other_ref) | copy-start | bytes 786436
  65.7 3.8 %copy-start = (bf16[8,128,512]{2,1,0:T(8,128)(2,1)}, bf16[8,128,512]{2,1,0:T(8,128)(2,1)S(1)}, u32[]{:S(2)}) copy-start(bf16[8,128,512]{2,1,0:T(8,128)(2,1)S(1)} %all-to-all-done.1) | copy-start | bytes 3145732
  65.7 80.1 %all-to-all-start = ((bf16[8,128,512]{2,1,0:T(8,128)(2,1)}), bf16[8,128,512]{2,1,0:T(8,128)(2,1)S(1)}, u32[]{:S(2)}, u32[]{:S(2)}) async-start(bf16[8,128,512]{2,1,0:T(8,128)(2,1)} %shard_map.119), calls=%async_computation | async-start | bytes 2097152 | tf_op jit(solution)/shard_map/all_to_all | solution.py:199
  72.6 65.3 %collective-permute-start.1 = (bf16[256,512]{1,0:T(8,128)(2,1)}, bf16[256,512]{1,0:T(8,128)(2,1)S(1)}, u32[]{:S(2)}, u32[]{:S(2)}) collective-permute-start(bf16[256,512]{1,0:T(8,128)(2,1)} %get-tuple-element.16), channel_id=1, source_target_pairs={{0,8},{8,0},{1,9},{9,1},{2,10},{10,2},{3,11},{11,3},{4,12},{12,4},... | collective-permute-start | bytes 786440 | tf_op jit(solution)/shard_map/ppermute | solution.py:209
  122.7 18.2 %collective-permute-start.5 = (bf16[64,768]{1,0:T(8,128)(2,1)}, bf16[64,768]{1,0:T(8,128)(2,1)S(1)}, u32[]{:S(2)}, u32[]{:S(2)}) collective-permute-start(bf16[64,768]{1,0:T(8,128)(2,1)} %shard_map.126.own_ref), channel_id=1, source_target_pairs={{0,384},{16,400},{384,0},{400,16},{1,385},{17,401},{385,1},{401,17... | collective-permute-start | bytes 294920 | tf_op jit(solution)/shard_map/ppermute | solution.py:219
  125.7 15.2 %collective-permute-start.6 = (bf16[64,768]{1,0:T(8,128)(2,1)}, bf16[64,768]{1,0:T(8,128)(2,1)S(1)}, u32[]{:S(2)}, u32[]{:S(2)}) collective-permute-start(bf16[64,768]{1,0:T(8,128)(2,1)} %shard_map.126.own_ref), channel_id=1, source_target_pairs={{0,16},{16,0},{384,400},{400,384},{1,17},{17,1},{385,401},{401,385... | collective-permute-start | bytes 294920 | tf_op jit(solution)/shard_map/ppermute | solution.py:219
  135.7 6.5 %collective-permute-start.7 = (bf16[64,768]{1,0:T(8,128)(2,1)}, bf16[64,768]{1,0:T(8,128)(2,1)S(1)}, u32[]{:S(2)}, u32[]{:S(2)}) collective-permute-start(bf16[64,768]{1,0:T(8,128)(2,1)} %shard_map.126.own_ref), channel_id=1, source_target_pairs={{0,400},{16,384},{384,16},{400,0},{1,401},{17,385},{385,17},{401,1... | collective-permute-start | bytes 294920 | tf_op jit(solution)/shard_map/ppermute | solution.py:219
  137.9 0.7 copy-start.3
  140.9 1.3 copy-start.5
  140.9 1.3 copy-start.6
  142.2 0.6 copy-start.7
  145.8 1.0 copy-start.1
Sparse Core Ops, SparseCore 0:
  10.3 51.5 all-gather.4
  64.3 56.2 all-gather.6

commit v4 on v1

v4 whole, which is shorter than its diff:
```python
import jax
import jax.numpy as jnp
from jax import lax
from jax.experimental import pallas as pl
from jax.experimental.pallas import tpu as pltpu
from jax.sharding import Mesh, PartitionSpec as P


AXES = ("x_lo", "z", "core", "x_hi", "y_hi", "y_lo")
REPLICA = AXES[:3]
FSDP = AXES[3:]
GROUP = ("x_hi", "y_lo")
f32, bf16 = jnp.float32, jnp.bfloat16
ROWS = 16


def whole():
    return pl.BlockSpec(memory_space=pltpu.VMEM)


def scalar():
    return pl.BlockSpec(memory_space=pltpu.SMEM)


def call(kernel, out_shape, operands, flops=0):
    outs = out_shape if isinstance(out_shape, (tuple, list)) else (out_shape,)
    moved = sum(a.size * a.dtype.itemsize for a in (*operands, *outs))
    return pl.pallas_call(
        kernel,
        out_shape=out_shape,
        in_specs=[scalar() if a.dtype == jnp.int32 else whole() for a in operands],
        out_specs=jax.tree.map(lambda _: whole(), out_shape),
        cost_estimate=pl.CostEstimate(flops=flops, bytes_accessed=moved, transcendentals=0),
    )(*operands)


def shape(dims, dtype):
    return jax.ShapeDtypeStruct(dims, dtype)


def inverse_of(rows):
    return lax.rsqrt(jnp.mean(rows * rows, axis=1, keepdims=True) + 1e-05)


PIECE = 256


def pieces(group_ref, step):
    member = lax.bitwise_xor(group_ref[0], step)
    start = lax.shift_right_logical(member, 1) * 2048 + lax.bitwise_and(member, 1) * PIECE
    return [pl.ds(pl.multiple_of(start + at * 2 * PIECE, PIECE), PIECE) for at in range(4)]


def norm_kernel(group_ref, hidden_ref, value_ref, scales_ref, *out_refs):
    def step(index, _):
        at = pl.ds(pl.multiple_of(index * ROWS, ROWS), ROWS)
        inverse = inverse_of(hidden_ref[at, :].astype(f32))
        for away in (1, 2, 3, 0):
            for place, columns in enumerate(pieces(group_ref, away)):
                unit = hidden_ref[at, columns].astype(f32) * inverse
                normed = (unit * scales_ref[:, columns]).astype(bf16)
                out_refs[away][at, pl.ds(place * PIECE, PIECE)] = normed
        return 0

    lax.fori_loop(0, hidden_ref.shape[0] // ROWS, step, 0)
    for ref in out_refs[1:]:
        ref[:, 4 * PIECE :] = value_ref[...]


def term_kernel(kept_ref, value_ref, first_ref, second_ref, third_ref, out_ref):
    across = (((0,), (0,)), ((), ()))
    for at in range(4):
        columns = slice(at * PIECE, (at + 1) * PIECE)
        total = lax.dot_general(
            kept_ref[:, columns], value_ref[...], across, preferred_element_type=f32
        )
        for ref in (first_ref, second_ref, third_ref):
            total += lax.dot_general(
                ref[:, columns], ref[:, 4 * PIECE :], across, preferred_element_type=f32
            )
        out_ref[columns, :] = total.astype(bf16)


def grad_kernel(weight_ref, first_ref, second_ref, third_ref, *out_refs):
    weight = weight_ref[...]
    for ref, out_ref in zip((first_ref, second_ref, third_ref), out_refs):
        out_ref[...] = lax.dot_general(
            ref[:, 4 * PIECE :], weight, (((1,), (1,)), ((), ())), preferred_element_type=f32
        ).astype(bf16)


def gain_kernel(place_ref, grad_ref, weight_ref, scales_ref, gain_ref):
    rows = grad_ref.shape[0]
    products = weight_ref[...].astype(f32) * grad_ref[...].astype(f32)
    sums = lax.dot_general(
        jnp.ones((8, products.shape[1]), f32),
        products,
        (((1,), (1,)), ((), ())),
        precision=lax.Precision.HIGHEST,
        preferred_element_type=f32,
    )
    columns = pl.ds(pl.multiple_of(place_ref[0] * rows, rows), rows)
    gain_ref[...] = sums[:1, :] / scales_ref[:, columns]


def pseudo_kernel(outer_ref, inner_ref, out_ref):
    for at in range(out_ref.shape[0]):
        columns = slice(at * 128, (at + 1) * 128)
        out_ref[at] = (outer_ref[:, columns] - inner_ref[:, columns]).astype(bf16)


def block_kernel(spread_ref, out_ref):
    count = spread_ref.shape[0]
    total = spread_ref[0].astype(f32)
    for at in range(1, count):
        total += spread_ref[at].astype(f32)
    mean = (total / count).astype(bf16)
    for at in range(count):
        out_ref[at] = mean


def outer_kernel(shared_ref, outer_ref, momentum_ref, new_outer_ref, new_momentum_ref):
    for at in range(shared_ref.shape[0]):
        columns = slice(at * 128, (at + 1) * 128)
        average = shared_ref[at].astype(f32)
        new_momentum = 0.9 * momentum_ref[:, columns] + average
        new_momentum_ref[:, columns] = new_momentum
        new_outer_ref[:, columns] = outer_ref[:, columns] - 0.7 * (average + 0.9 * new_momentum)


def hidden_kernel(
    group_ref, hidden_ref, res_ref, scales_ref, own_ref, first_ref, second_ref, third_ref, out_ref
):
    def step(index, _):
        at = pl.ds(pl.multiple_of(index * ROWS, ROWS), ROWS)
        inverse = inverse_of(hidden_ref[at, :].astype(f32))

        def parts():
            for away, ref in enumerate((own_ref, first_ref, second_ref, third_ref)):
                for place, columns in enumerate(pieces(group_ref, away)):
                    grad = ref[at, pl.ds(place * PIECE, PIECE)].astype(f32)
                    scaled = grad * scales_ref[:, columns]
                    yield columns, scaled, hidden_ref[at, columns].astype(f32) * inverse

        total = jnp.zeros((ROWS, PIECE), f32)
        for _, scaled, unit in parts():
            total += scaled * unit
        projection = jnp.sum(total, axis=1, keepdims=True) / hidden_ref.shape[1]
        for columns, scaled, unit in parts():
            grad = res_ref[at, columns].astype(f32) + inverse * (scaled - unit * projection)
            out_ref[at, columns] = grad.astype(bf16)
        return 0

    lax.fori_loop(0, hidden_ref.shape[0] // ROWS, step, 0)


def body(
    hidden_in, res_grad, value_grad, value_weight, norm_gain, inner_frag, outer_frag, momentum
):
    group = lax.axis_index(GROUP).reshape(1)
    own_weight = value_weight[0]
    tokens, width = hidden_in.shape
    features = value_grad.shape[1]
    quarter = width // 4
    weights = lax.all_gather(own_weight, "y_hi", axis=0, tiled=True)

    def trade(parts):
        received = []
        for step, part in enumerate(parts, 1):
            table = [(at, at ^ step) for at in range(4)]
            received.append(lax.ppermute(part, GROUP, table))
        return received

    kept, *sent = call(
        norm_kernel,
        (shape((tokens, quarter), bf16),) + (shape((tokens, quarter + features), bf16),) * 3,
        (group, hidden_in, value_grad, norm_gain),
    )
    received = trade(sent)
    term = call(term_kernel, shape((quarter, features), bf16), (kept, value_grad, *received))
    weight_grad = lax.psum_scatter(term, "y_hi", scatter_dimension=0, tiled=True)

    rows, columns = outer_frag.shape
    split = (columns // 128, rows, 128)
    pseudo_grad = call(
        pseudo_kernel, shape(split, bf16), (outer_frag, inner_frag[0])
    ).reshape(48, -1, 128)
    spread = lax.all_to_all(pseudo_grad, REPLICA, 0, 0)
    block = call(block_kernel, shape(spread.shape, bf16), (spread,))
    shared = lax.all_to_all(block, REPLICA, 0, 0)
    new_outer, new_momentum = call(
        outer_kernel,
        (shape(outer_frag.shape, f32), shape(outer_frag.shape, f32)),
        (shared.reshape(split), outer_frag, momentum),
    )

    grads = call(grad_kernel, (shape((tokens, quarter), bf16),) * 3, (weights, *received))
    grads = trade(grads)
    own_grad = lax.dot_general(
        value_grad, weights, (((1,), (1,)), ((), ())), preferred_element_type=f32
    )
    hidden_grad = call(
        hidden_kernel,
        shape(hidden_in.shape, bf16),
        (group, hidden_in, res_grad, norm_gain, own_grad, *grads),
    )
    gain_grad = call(
        gain_kernel,
        shape((1, own_weight.shape[0]), f32),
        (lax.axis_index(FSDP).reshape(1), weight_grad, own_weight, norm_gain),
    )
    return (hidden_grad, weight_grad[None], gain_grad, new_outer, new_momentum)


def solution(mesh):
    grid = Mesh(mesh.devices.reshape(2, 12, 2, 2, 4, 2), AXES)
    in_specs = (
        P(AXES, None),
        P(AXES, None),
        P(AXES, None),
        P(REPLICA, FSDP, None),
        P(REPLICA, None),
        P(REPLICA, FSDP, None),
        P(FSDP, None),
        P(FSDP, None),
    )
    out_specs = (
        P(AXES, None),
        P(REPLICA, FSDP, None),
        P(REPLICA, FSDP),
        P(FSDP, None),
        P(FSDP, None),
    )

    def step(*arrays):
        return body(*arrays)

    step = jax.shard_map(step, mesh=grid, in_specs=in_specs, out_specs=out_specs, check_vma=False)
    return step
```

time: 123 us -> 128 us (1.041)
  the two profiles are of different devices: /device:TPU:6 before, /device:TPU:16 now
where the time goes in v4:
time: 128 us
  starting transfers between devices  47.9 us (37%)
  waiting for transfers between devices  36.2 us (28%)
  Pallas kernels  24.8 us (19%)
  between operations  14.2 us (11%)
  local copies, waits for them, and re-layouts  3.19 us (2%)
    pallas_call x8, Pallas kernels, call(): pl.pallas_call(kernel, out_shape=out_shape, in_specs=[scalar() if a.dtype...  24.8 us
    ppermute x6, starting transfers between devices, trade(): received.append(lax.ppermute(part, GROUP, table))  23.7 us
    ppermute x6, waiting for transfers between devices, trade(): received.append(lax.ppermute(part, GROUP, table))  22.6 us
    all_to_all x1, starting transfers between devices, body(): spread = lax.all_to_all(pseudo_grad, REPLICA, 0, 0)  16.8 us
    all_to_all x1, waiting for transfers between devices, body(): spread = lax.all_to_all(pseudo_grad, REPLICA, 0, 0)  12.9 us
    all_to_all x1, starting transfers between devices, body(): shared = lax.all_to_all(block, REPLICA, 0, 0)  7.42 us
    unnamed x20, local copies, waits for them, and re-layouts  3.19 us
  transfers between devices with their start and end apart: 10, of which 3 were waited for; matrix products, arithmetic and copies ran while one was open for 1% of the time, Pallas kernels for 18%

profile of v4, /device:TPU:16, one launch (start us, length us, event | category | flops | bytes accessed | tf_op | source)
XLA Modules:
  0.0 127.6 jit_solution(8384611318577098312)
XLA Ops:
  7.2 0.0 all-gather.3.cloned.1.call-start
  7.2 0.7 all-gather.3.cloned.1.call-update
  7.9 3.6 %shard_map.119 = (bf16[128,1024]{1,0:T(8,128)(2,1)}, bf16[128,1536]{1,0:T(8,128)(2,1)}, bf16[128,1536]{1,0:T(8,128)(2,1)}, bf16[128,1536]{1,0:T(8,128)(2,1)}) custom-call(s32[1]{0:T(128)} %bitcast.group_ref, bf16[128,4096]{1,0:T(8,128)(2,1)} %hidden_ref.3, bf16[128,512]{1,0:T(8,128)(2,1)} %value_ref.3, f32[1,4096]{1,0:T(1,128)} %scales_ref.5), custom_call_target="tpu_custom_call" | custom-call | bytes 2637828 | tf_op jit(solution)/shard_map/pallas_call | solution.py:28
  11.5 3.5 %collective-permute-start = (bf16[128,1536]{1,0:T(8,128)(2,1)}, bf16[128,1536]{1,0:T(8,128)(2,1)S(1)}, u32[]{:S(2)}, u32[]{:S(2)}) collective-permute-start(bf16[128,1536]{1,0:T(8,128)(2,1)} %get-tuple-element.14), channel_id=1, source_target_pairs={{0,1},{1,0},{8,9},{9,8},{2,3},{3,2},{10,11},{11,10},{4,5},{5,4},{1... | collective-permute-start | bytes 1179656 | tf_op jit(solution)/shard_map/ppermute | solution.py:171
  15.0 4.9 %collective-permute-start.1 = (bf16[128,1536]{1,0:T(8,128)(2,1)}, bf16[128,1536]{1,0:T(8,128)(2,1)S(1)}, u32[]{:S(2)}, u32[]{:S(2)}) collective-permute-start(bf16[128,1536]{1,0:T(8,128)(2,1)} %get-tuple-element.15), channel_id=1, source_target_pairs={{0,8},{1,9},{8,0},{9,1},{2,10},{3,11},{10,2},{11,3},{4,12},{5,13},... | collective-permute-start | bytes 1179656 | tf_op jit(solution)/shard_map/ppermute | solution.py:171
  19.9 2.3 %collective-permute-start.2 = (bf16[128,1536]{1,0:T(8,128)(2,1)}, bf16[128,1536]{1,0:T(8,128)(2,1)S(1)}, u32[]{:S(2)}, u32[]{:S(2)}) collective-permute-start(bf16[128,1536]{1,0:T(8,128)(2,1)} %get-tuple-element.16), channel_id=1, source_target_pairs={{0,9},{1,8},{8,1},{9,0},{2,11},{3,10},{10,3},{11,2},{4,13},{5,12},... | collective-permute-start | bytes 1179656 | tf_op jit(solution)/shard_map/ppermute | solution.py:171
  22.2 2.2 %shard_map.124 = bf16[6,256,128]{2,1,0:T(8,128)(2,1)} custom-call(f32[256,768]{1,0:T(8,128)} %outer_ref.3, f32[256,768]{1,0:T(8,128)} %bitcast.15), custom_call_target="tpu_custom_call" | custom-call | bytes 1966080 | tf_op jit(solution)/shard_map/pallas_call | solution.py:28
  24.4 16.8 %all-to-all-start = ((bf16[48,32,128]{2,1,0:T(8,128)(2,1)}), bf16[48,32,128]{2,1,0:T(8,128)(2,1)S(1)}, u32[]{:S(2)}, u32[]{:S(2)}) async-start(bf16[48,32,128]{2,1,0:T(8,128)(2,1)} %bitcast.13), calls=%async_computation.1 | async-start | bytes 786432 | tf_op jit(solution)/shard_map/all_to_all | solution.py:188
  41.2 0.0 reduce-scatter.2.cloned.1.call-start
  41.3 0.0 copy-start.3
  41.3 0.7 copy-done.2
  42.0 0.1 copy-done.3
  42.1 0.1 copy-done.4
  42.3 3.7 %shard_map.122 = bf16[1024,512]{1,0:T(8,128)(2,1)} custom-call(bf16[128,1024]{1,0:T(8,128)(2,1)} %get-tuple-element.20.kept_ref, bf16[128,512]{1,0:T(8,128)(2,1)} %value_ref.3, bf16[128,1536]{1,0:T(8,128)(2,1)} %copy-done.2, bf16[128,1536]{1,0:T(8,128)(2,1)} %copy-done.3, bf16[128,1536]{1,0:T(8,128)(2,1)} %copy-done.4), custom_call_target="tpu_custom_call" | custom-call | bytes 2621440 | tf_op jit(solution)/shard_map/pallas_call | solution.py:28
  45.9 0.0 reduce-scatter.2.cloned.1.call-update
  46.0 12.9 %all-to-all-done.spread_ref = bf16[48,32,128]{2,1,0:T(8,128)(2,1)S(1)} async-done(((bf16[48,32,128]{2,1,0:T(8,128)(2,1)}), bf16[48,32,128]{2,1,0:T(8,128)(2,1)S(1)}, u32[]{:S(2)}, u32[]{:S(2)}) %all-to-all-start) | async-done | bytes 393248 | tf_op jit(solution)/shard_map/all_to_all | solution.py:188
  58.8 0.8 copy-done.1
  59.6 1.8 %shard_map.125 = bf16[48,32,128]{2,1,0:T(8,128)(2,1)} custom-call(bf16[48,32,128]{2,1,0:T(8,128)(2,1)} %copy-done.1), custom_call_target="tpu_custom_call" | custom-call | bytes 786432 | tf_op jit(solution)/shard_map/pallas_call | solution.py:28
  61.4 7.4 %all-to-all-start.1 = ((bf16[48,32,128]{2,1,0:T(8,128)(2,1)}), bf16[48,32,128]{2,1,0:T(8,128)(2,1)S(1)}, u32[]{:S(2)}, u32[]{:S(2)}) async-start(bf16[48,32,128]{2,1,0:T(8,128)(2,1)} %shard_map.125), calls=%async_computation.2 | async-start | bytes 786432 | tf_op jit(solution)/shard_map/all_to_all | solution.py:190
  68.9 0.0 all-gather.3.cloned.1.call-done
  68.9 3.5 %shard_map.120 = (bf16[128,1024]{1,0:T(8,128)(2,1)}, bf16[128,1024]{1,0:T(8,128)(2,1)}, bf16[128,1024]{1,0:T(8,128)(2,1)}) custom-call(bf16[1024,512]{1,0:T(8,128)(2,1)} %bitcast.11, bf16[128,1536]{1,0:T(8,128)(2,1)} %copy-done.2, bf16[128,1536]{1,0:T(8,128)(2,1)} %copy-done.3, bf16[128,1536]{1,0:T(8,128)(2,1)} %copy-done.4), custom_call_target="tpu_custom_call" | custom-call | bytes 3014656 | tf_op jit(solution)/shard_map/pallas_call | solution.py:28
  72.4 6.2 %collective-permute-start.3 = (bf16[128,1024]{1,0:T(8,128)(2,1)}, bf16[128,1024]{1,0:T(8,128)(2,1)S(1)}, u32[]{:S(2)}, u32[]{:S(2)}) collective-permute-start(bf16[128,1024]{1,0:T(8,128)(2,1)} %get-tuple-element.17), channel_id=1, source_target_pairs={{0,1},{1,0},{8,9},{9,8},{2,3},{3,2},{10,11},{11,10},{4,5},{5,4},{1... | collective-permute-start | bytes 786440 | tf_op jit(solution)/shard_map/ppermute | solution.py:171
  78.6 3.9 %collective-permute-start.4 = (bf16[128,1024]{1,0:T(8,128)(2,1)}, bf16[128,1024]{1,0:T(8,128)(2,1)S(1)}, u32[]{:S(2)}, u32[]{:S(2)}) collective-permute-start(bf16[128,1024]{1,0:T(8,128)(2,1)} %get-tuple-element.18), channel_id=1, source_target_pairs={{0,8},{1,9},{8,0},{9,1},{2,10},{3,11},{10,2},{11,3},{4,12},{5,13},... | collective-permute-start | bytes 786440 | tf_op jit(solution)/shard_map/ppermute | solution.py:171
  82.5 2.9 %collective-permute-start.5 = (bf16[128,1024]{1,0:T(8,128)(2,1)}, bf16[128,1024]{1,0:T(8,128)(2,1)S(1)}, u32[]{:S(2)}, u32[]{:S(2)}) collective-permute-start(bf16[128,1024]{1,0:T(8,128)(2,1)} %get-tuple-element.19), channel_id=1, source_target_pairs={{0,9},{1,8},{8,1},{9,0},{2,11},{3,10},{10,3},{11,2},{4,13},{5,12},... | collective-permute-start | bytes 786440 | tf_op jit(solution)/shard_map/ppermute | solution.py:171
  85.4 1.3 fusion.own_ref
  86.7 11.6 %collective-permute-done.3.first_ref = bf16[128,1024]{1,0:T(8,128)(2,1)S(1)} collective-permute-done((bf16[128,1024]{1,0:T(8,128)(2,1)}, bf16[128,1024]{1,0:T(8,128)(2,1)S(1)}, u32[]{:S(2)}, u32[]{:S(2)}) %collective-permute-start.3) | collective-permute-done | bytes 262176 | tf_op jit(solution)/shard_map/ppermute | solution.py:171
  98.2 11.0 %collective-permute-done.5.third_ref = bf16[128,1024]{1,0:T(8,128)(2,1)S(1)} collective-permute-done((bf16[128,1024]{1,0:T(8,128)(2,1)}, bf16[128,1024]{1,0:T(8,128)(2,1)S(1)}, u32[]{:S(2)}, u32[]{:S(2)}) %collective-permute-start.5) | collective-permute-done | bytes 262176 | tf_op jit(solution)/shard_map/ppermute | solution.py:171
  109.3 0.7 copy-done.9
  110.0 5.0 %shard_map.121 = bf16[128,4096]{1,0:T(8,128)(2,1)} custom-call(s32[1]{0:T(128)} %bitcast.group_ref, bf16[128,4096]{1,0:T(8,128)(2,1)} %hidden_ref.3, bf16[128,4096]{1,0:T(8,128)(2,1)} %res_ref.1, f32[1,4096]{1,0:T(1,128)} %scales_ref.5, f32[128,1024]{1,0:T(8,128)} %fusion.own_ref, bf16[128,1024]{1,0:T(8,128)(2,1)} %copy-done.7, bf16[128,1024]{1,0:T(8,128)(2,1)} %copy-done.8, ...), custom_call_target="tpu_custom_call" | custom-call | bytes 4472836 | tf_op jit(solution)/shard_map/pallas_call | solution.py:28
  115.0 0.7 copy-done.5
  115.8 2.8 %shard_map.126 = (f32[256,768]{1,0:T(8,128)}, f32[256,768]{1,0:T(8,128)}) custom-call(bf16[6,256,128]{2,1,0:T(8,128)(2,1)} %bitcast.12, f32[256,768]{1,0:T(8,128)} %outer_ref.3, f32[256,768]{1,0:T(8,128)} %momentum_ref.1), custom_call_target="tpu_custom_call" | custom-call | bytes 3538944 | tf_op jit(solution)/shard_map/pallas_call | solution.py:28
  118.6 2.1 %shard_map.123 = f32[1,256]{1,0:T(1,128)} custom-call(s32[1]{0:T(128)} %bitcast.3.place_ref, bf16[256,512]{1,0:T(8,128)(2,1)} %reduce-scatter.2.cloned.1.call-done.grad_ref, bf16[256,512]{1,0:T(8,128)(2,1)} %bitcast.14, f32[1,4096]{1,0:T(1,128)} %scales_ref.5), custom_call_target="tpu_custom_call" | custom-call | bytes 541700 | tf_op jit(solution)/shard_map/pallas_call | solution.py:28
  (19 shorter events, 0.0 us)
Async XLA Ops:
  7.2 61.7 %all-gather.3.cloned.1.call-start = ((), (), s32[]{:S(2)}) async-start(), calls=%async_computation.4 | async-start | bytes 1310720 | tf_op jit(solution)/shard_map/all_gather | solution.py:165
  11.5 29.7 %collective-permute-start = (bf16[128,1536]{1,0:T(8,128)(2,1)}, bf16[128,1536]{1,0:T(8,128)(2,1)S(1)}, u32[]{:S(2)}, u32[]{:S(2)}) collective-permute-start(bf16[128,1536]{1,0:T(8,128)(2,1)} %get-tuple-element.14), channel_id=1, source_target_pairs={{0,1},{1,0},{8,9},{9,8},{2,3},{3,2},{10,11},{11,10},{4,5},{5,4},{1... | collective-permute-start | bytes 1179656 | tf_op jit(solution)/shard_map/ppermute | solution.py:171
  15.0 26.3 %collective-permute-start.1 = (bf16[128,1536]{1,0:T(8,128)(2,1)}, bf16[128,1536]{1,0:T(8,128)(2,1)S(1)}, u32[]{:S(2)}, u32[]{:S(2)}) collective-permute-start(bf16[128,1536]{1,0:T(8,128)(2,1)} %get-tuple-element.15), channel_id=1, source_target_pairs={{0,8},{1,9},{8,0},{9,1},{2,10},{3,11},{10,2},{11,3},{4,12},{5,13},... | collective-permute-start | bytes 1179656 | tf_op jit(solution)/shard_map/ppermute | solution.py:171
  19.9 21.4 %collective-permute-start.2 = (bf16[128,1536]{1,0:T(8,128)(2,1)}, bf16[128,1536]{1,0:T(8,128)(2,1)S(1)}, u32[]{:S(2)}, u32[]{:S(2)}) collective-permute-start(bf16[128,1536]{1,0:T(8,128)(2,1)} %get-tuple-element.16), channel_id=1, source_target_pairs={{0,9},{1,8},{8,1},{9,0},{2,11},{3,10},{10,3},{11,2},{4,13},{5,12},... | collective-permute-start | bytes 1179656 | tf_op jit(solution)/shard_map/ppermute | solution.py:171
  24.4 34.4 %all-to-all-start = ((bf16[48,32,128]{2,1,0:T(8,128)(2,1)}), bf16[48,32,128]{2,1,0:T(8,128)(2,1)S(1)}, u32[]{:S(2)}, u32[]{:S(2)}) async-start(bf16[48,32,128]{2,1,0:T(8,128)(2,1)} %bitcast.13), calls=%async_computation.1 | async-start | bytes 786432 | tf_op jit(solution)/shard_map/all_to_all | solution.py:188
  41.2 77.4 %reduce-scatter.2.cloned.1.call-start = ((), (), s32[]{:S(2)}) async-start(), calls=%async_computation.3 | async-start | bytes 1310720 | tf_op jit(solution)/shard_map/reduce_scatter | solution.py:181
  41.3 0.7 copy-start.2
  41.3 0.9 copy-start.3
  41.3 1.0 copy-start.4
  58.8 0.8 copy-start.1
  61.4 53.6 %all-to-all-start.1 = ((bf16[48,32,128]{2,1,0:T(8,128)(2,1)}), bf16[48,32,128]{2,1,0:T(8,128)(2,1)S(1)}, u32[]{:S(2)}, u32[]{:S(2)}) async-start(bf16[48,32,128]{2,1,0:T(8,128)(2,1)} %shard_map.125), calls=%async_computation.2 | async-start | bytes 786432 | tf_op jit(solution)/shard_map/all_to_all | solution.py:190
  68.9 16.5 %copy-start = (bf16[1,1024,512]{2,1,0:T(8,128)(2,1)S(1)}, bf16[1,1024,512]{2,1,0:T(8,128)(2,1)}, u32[]{:S(2)}) copy-start(bf16[1,1024,512]{2,1,0:T(8,128)(2,1)} %all-gather.3.cloned.1.call-done) | copy-start | bytes 3145732
  68.9 16.5 %copy-start.6 = (bf16[128,512]{1,0:T(8,128)(2,1)S(1)}, bf16[128,512]{1,0:T(8,128)(2,1)}, u32[]{:S(2)}) copy-start(bf16[128,512]{1,0:T(8,128)(2,1)} %value_ref.3) | copy-start | bytes 393220
  72.4 25.8 %collective-permute-start.3 = (bf16[128,1024]{1,0:T(8,128)(2,1)}, bf16[128,1024]{1,0:T(8,128)(2,1)S(1)}, u32[]{:S(2)}, u32[]{:S(2)}) collective-permute-start(bf16[128,1024]{1,0:T(8,128)(2,1)} %get-tuple-element.17), channel_id=1, source_target_pairs={{0,1},{1,0},{8,9},{9,8},{2,3},{3,2},{10,11},{11,10},{4,5},{5,4},{1... | collective-permute-start | bytes 786440 | tf_op jit(solution)/shard_map/ppermute | solution.py:171
  78.6 19.7 %collective-permute-start.4 = (bf16[128,1024]{1,0:T(8,128)(2,1)}, bf16[128,1024]{1,0:T(8,128)(2,1)S(1)}, u32[]{:S(2)}, u32[]{:S(2)}) collective-permute-start(bf16[128,1024]{1,0:T(8,128)(2,1)} %get-tuple-element.18), channel_id=1, source_target_pairs={{0,8},{1,9},{8,0},{9,1},{2,10},{3,11},{10,2},{11,3},{4,12},{5,13},... | collective-permute-start | bytes 786440 | tf_op jit(solution)/shard_map/ppermute | solution.py:171
  82.5 26.8 %collective-permute-start.5 = (bf16[128,1024]{1,0:T(8,128)(2,1)}, bf16[128,1024]{1,0:T(8,128)(2,1)S(1)}, u32[]{:S(2)}, u32[]{:S(2)}) collective-permute-start(bf16[128,1024]{1,0:T(8,128)(2,1)} %get-tuple-element.19), channel_id=1, source_target_pairs={{0,9},{1,8},{8,1},{9,0},{2,11},{3,10},{10,3},{11,2},{4,13},{5,12},... | collective-permute-start | bytes 786440 | tf_op jit(solution)/shard_map/ppermute | solution.py:171
  98.2 11.1 %copy-start.7 = (bf16[128,1024]{1,0:T(8,128)(2,1)}, bf16[128,1024]{1,0:T(8,128)(2,1)S(1)}, u32[]{:S(2)}) copy-start(bf16[128,1024]{1,0:T(8,128)(2,1)S(1)} %collective-permute-done.3.first_ref) | copy-start | bytes 786436
  98.2 11.1 %copy-start.8 = (bf16[128,1024]{1,0:T(8,128)(2,1)}, bf16[128,1024]{1,0:T(8,128)(2,1)S(1)}, u32[]{:S(2)}) copy-start(bf16[128,1024]{1,0:T(8,128)(2,1)S(1)} %collective-permute-done.4.second_ref) | copy-start | bytes 786436
  109.3 0.7 copy-start.9
  115.0 0.7 copy-start.5
Sparse Core Ops, SparseCore 0:
  10.4 46.2 all-gather.2
  60.3 45.5 reduce-scatter.1

commit v5 on v1

--- a/solution.py
+++ b/solution.py
@@ -6,7 +6,7 @@
 from jax.sharding import Mesh, PartitionSpec as P
 
 
-AXES = ("x_lo", "z", "core", "x_hi", "y")
+AXES = ("x_lo", "z", "core", "x_hi", "y_hi", "y_lo")
 REPLICA = AXES[:3]
 FSDP = AXES[3:]
 SWAP = [(0, 1), (1, 0)]
@@ -42,22 +42,31 @@
     return lax.rsqrt(jnp.mean(rows * rows, axis=1, keepdims=True) + 1e-05)
 
 
-def norm_kernel(upper_ref, hidden_ref, scales_ref, kept_ref, sent_ref):
+def pair_kernel(parity_ref, own_ref, other_ref, out_ref):
+    out_ref[parity_ref[0]] = own_ref[...]
+    out_ref[1 - parity_ref[0]] = other_ref[...]
+
+
+def sides(upper_ref, half):
+    return [
+        pl.ds(pl.multiple_of(side * half, half), half) for side in (upper_ref[0], 1 - upper_ref[0])
+    ]
+
+
+def norm_kernel(upper_ref, hidden_ref, scales_ref, kept_ref, sent_ref, inverse_ref):
     tokens, width = hidden_ref.shape
-    half = width // 2
-    own = pl.multiple_of(upper_ref[0] * half, half)
-    other = pl.multiple_of((1 - upper_ref[0]) * half, half)
+    own, other = sides(upper_ref, width // 2)
 
     def step(index, _):
         at = pl.ds(pl.multiple_of(index * ROWS, ROWS), ROWS)
         inverse = inverse_of(hidden_ref[at, :].astype(f32))
-        for start, target in ((other, sent_ref), (own, kept_ref)):
-            columns = pl.ds(start, half)
+        inverse_ref[at, :] = jnp.broadcast_to(inverse, (ROWS, 128))
+        for columns, target in ((other, sent_ref), (own, kept_ref)):
             unit = hidden_ref[at, columns].astype(f32) * inverse
             target[at, :] = (unit * scales_ref[:, columns]).astype(bf16)
         return 0
 
-    lax.fori_loop(0, tokens // ROWS, step, 0)
+    lax.fori_loop(0, tokens // ROWS, step, 0, unroll=2)
 
 
 def pseudo_kernel(outer_ref, inner_ref, out_ref):
@@ -85,32 +94,41 @@
         new_outer_ref[:, columns] = outer_ref[:, columns] - 0.7 * (average + 0.9 * new_momentum)
 
 
-def hidden_kernel(upper_ref, hidden_ref, res_ref, scales_ref, own_ref, other_ref, out_ref):
+def hidden_kernel(
+    upper_ref, hidden_ref, res_ref, scales_ref, inverse_ref, own_ref, other_ref, out_ref
+):
     tokens, width = hidden_ref.shape
-    half = width // 2
-    own = pl.multiple_of(upper_ref[0] * half, half)
-    other = pl.multiple_of((1 - upper_ref[0]) * half, half)
+    parts = tuple(zip(sides(upper_ref, width // 2), (own_ref, other_ref)))
 
     def step(index, _):
         at = pl.ds(pl.multiple_of(index * ROWS, ROWS), ROWS)
-        inverse = inverse_of(hidden_ref[at, :].astype(f32))
+        inverse = inverse_ref[at, :][:, :1]
         total = jnp.zeros((ROWS, 1), f32)
-        parts = ((own, own_ref), (other, other_ref))
-        for start, grad_ref in parts:
-            columns = pl.ds(start, half)
+        for columns, grad_ref in parts:
             scaled = grad_ref[at, :].astype(f32) * scales_ref[:, columns]
-            unit = hidden_ref[at, columns].astype(f32) * inverse
-            total += jnp.sum(scaled * unit, axis=1, keepdims=True)
-        projection = total / width
-        for start, grad_ref in parts:
-            columns = pl.ds(start, half)
+            total += jnp.sum(scaled * hidden_ref[at, columns].astype(f32), axis=1, keepdims=True)
+        shift = inverse * (inverse * total / width)
+        for columns, grad_ref in parts:
             scaled = grad_ref[at, :].astype(f32) * scales_ref[:, columns]
-            unit = hidden_ref[at, columns].astype(f32) * inverse
-            grad = res_ref[at, columns].astype(f32) + inverse * (scaled - unit * projection)
-            out_ref[at, columns] = grad.astype(bf16)
+            inner = scaled - hidden_ref[at, columns].astype(f32) * shift
+            out_ref[at, columns] = (res_ref[at, columns].astype(f32) + inverse * inner).astype(bf16)
         return 0
 
-    lax.fori_loop(0, tokens // ROWS, step, 0)
+    lax.fori_loop(0, tokens // ROWS, step, 0, unroll=2)
+
+
+def gain_kernel(place_ref, grad_ref, weight_ref, scales_ref, gain_ref):
+    rows = grad_ref.shape[0]
+    products = weight_ref[...].astype(f32) * grad_ref[...].astype(f32)
+    sums = lax.dot_general(
+        jnp.ones((8, products.shape[1]), f32),
+        products,
+        (((1,), (1,)), ((), ())),
+        precision=lax.Precision.HIGHEST,
+        preferred_element_type=f32,
+    )
+    columns = pl.ds(pl.multiple_of(place_ref[0] * rows, rows), rows)
+    gain_ref[...] = sums[:1, :] / scales_ref[:, columns]
 
 
 def body(
@@ -120,12 +138,21 @@
     own_weight = value_weight[0]
     tokens, width = hidden_in.shape
     half = width // 2
-    weight_half = lax.all_gather(own_weight, "y", axis=0, tiled=True)
+    other_weight = lax.ppermute(own_weight, "y_lo", SWAP)
+    parity = lax.axis_index("y_lo").reshape(1)
+    weight_pair = call(
+        pair_kernel, shape((2, *own_weight.shape), bf16), (parity, own_weight, other_weight)
+    ).reshape(-1, own_weight.shape[1])
+    weight_half = lax.all_gather(weight_pair, "y_hi", axis=0, tiled=True)
     partner_value = lax.ppermute(value_grad, "x_hi", SWAP)
 
-    kept, sent = call(
+    kept, sent, inverse = call(
         norm_kernel,
-        (shape((tokens, half), bf16), shape((tokens, half), bf16)),
+        (
+            shape((tokens, half), bf16),
+            shape((tokens, half), bf16),
+            shape((tokens, 128), f32),
+        ),
         (upper, hidden_in, norm_gain),
     )
     received = lax.ppermute(sent, "x_hi", SWAP)
@@ -135,7 +162,9 @@
         (((0,), (0,)), ((), ())),
         preferred_element_type=f32,
     ).astype(bf16)
-    weight_grad = lax.psum_scatter(term, "y", scatter_dimension=0, tiled=True)
+    weight_grad = lax.psum_scatter(
+        term, ("y_hi", "y_lo"), scatter_dimension=0, tiled=True
+    )
 
     rows, columns = outer_frag.shape
     split = (columns // 128, rows, 128)
@@ -160,19 +189,19 @@
     hidden_grad = call(
         hidden_kernel,
         shape(hidden_in.shape, bf16),
-        (upper, hidden_in, res_grad, norm_gain, own_grad, other_grad),
-    )
-
-    count = own_weight.shape[0]
-    own_scales = lax.dynamic_slice_in_dim(norm_gain[0], lax.axis_index(FSDP) * count, count, 0)
-    gain_grad = (
-        jnp.sum(own_weight.astype(f32) * weight_grad.astype(f32), axis=1) / own_scales
-    )
-    return (hidden_grad, weight_grad[None], gain_grad[None], new_outer, new_momentum)
+        (upper, hidden_in, res_grad, norm_gain, inverse, own_grad, other_grad),
+    )
+
+    gain_grad = call(
+        gain_kernel,
+        shape((1, own_weight.shape[0]), f32),
+        (lax.axis_index(FSDP).reshape(1), weight_grad, own_weight, norm_gain),
+    )
+    return (hidden_grad, weight_grad[None], gain_grad, new_outer, new_momentum)
 
 
 def solution(mesh):
-    grid = Mesh(mesh.devices.reshape(2, 12, 2, 2, 8), AXES)
+    grid = Mesh(mesh.devices.reshape(2, 12, 2, 2, 4, 2), AXES)
     in_specs = (
         P(AXES, None),
         P(AXES, None),

time: 123 us -> 133 us (1.081)
  the two profiles are of different devices: /device:TPU:6 before, /device:TPU:1 now
where the time goes in v5:
time: 133 us; the launch traced here: 132 us
  blocking collectives  41.9 us (32%)
  starting transfers between devices  24.5 us (18%)
  waiting for transfers between devices  21.3 us (16%)
  Pallas kernels  18.1 us (14%)
  between operations  15.6 us (12%)
  matrix products  8.37 us (6%)
  local copies, waits for them, and re-layouts  2.25 us (2%)
    all_to_all x1, blocking collectives, body(): spread = lax.all_to_all(pseudo_grad, REPLICA, 0, 0)  41.9 us
    pallas_call x7, Pallas kernels, call(): pl.pallas_call(kernel, out_shape=out_shape, in_specs=[scalar() if a.dtype...  18.1 us
    all_to_all x1, waiting for transfers between devices, body(): shared = lax.all_to_all(block, REPLICA, 0, 0)  10.7 us
    all_to_all x1, starting transfers between devices, body(): shared = lax.all_to_all(block, REPLICA, 0, 0)  7.33 us
    ppermute x1, starting transfers between devices, body(): received = lax.ppermute(sent, 'x_hi', SWAP)  6.77 us
    ppermute x1, waiting for transfers between devices, body(): partner_value = lax.ppermute(value_grad, 'x_hi', SWAP)  6.51 us
    ppermute x1, starting transfers between devices, body(): other_grad = lax.ppermute(partner_grad, 'x_hi', SWAP)  4.35 us
    ppermute x1, starting transfers between devices, body(): other_weight = lax.ppermute(own_weight, 'y_lo', SWAP)  4.02 us
  transfers between devices with their start and end apart: 7, of which 3 were waited for; matrix products, arithmetic and copies ran while one was open for 6% of the time, Pallas kernels for 11%

profile of v5, /device:TPU:1, one launch (start us, length us, event | category | flops | bytes accessed | tf_op | source)
XLA Modules:
  0.0 131.9 jit_solution(13239284040487160727)
XLA Ops:
  8.0 0.0 copy-start.4
  8.0 0.0 all-gather.2.cloned.1.call-start
  8.1 4.0 %collective-permute-start = (bf16[256,512]{1,0:T(8,128)(2,1)}, bf16[256,512]{1,0:T(8,128)(2,1)S(1)}, u32[]{:S(2)}, u32[]{:S(2)}) collective-permute-start(bf16[256,512]{1,0:T(8,128)(2,1)} %bitcast.20), channel_id=1, source_target_pairs={{0,1},{1,0},{2,3},{3,2},{4,5},{5,4},{6,7},{7,6},{8,9},{9,8},{10,11... | collective-permute-start | bytes 786440 | tf_op jit(solution)/shard_map/ppermute | solution.py:141
  12.1 4.0 %collective-permute-done.other_ref = bf16[256,512]{1,0:T(8,128)(2,1)S(1)} collective-permute-done((bf16[256,512]{1,0:T(8,128)(2,1)}, bf16[256,512]{1,0:T(8,128)(2,1)S(1)}, u32[]{:S(2)}, u32[]{:S(2)}) %collective-permute-start) | collective-permute-done | bytes 262176 | tf_op jit(solution)/shard_map/ppermute | solution.py:141
  16.0 0.7 copy-done.3
  16.7 1.9 %shard_map.120 = bf16[2,256,512]{2,1,0:T(8,128)(2,1)} custom-call(s32[1]{0:T(128)} %bitcast.1.parity_ref, bf16[256,512]{1,0:T(8,128)(2,1)} %bitcast.21, bf16[256,512]{1,0:T(8,128)(2,1)} %copy-done.3), custom_call_target="tpu_custom_call" | custom-call | bytes 1048580 | tf_op jit(solution)/shard_map/pallas_call | solution.py:28
  18.6 0.0 all-gather.2.cloned.1.call-update
  18.6 0.0 reduce-scatter.2.cloned.1.call-start
  18.7 2.9 %shard_map.119 = (bf16[128,2048]{1,0:T(8,128)(2,1)}, bf16[128,2048]{1,0:T(8,128)(2,1)}, f32[128,128]{1,0:T(8,128)}) custom-call(s32[1]{0:T(128)} %bitcast.upper_ref, bf16[128,4096]{1,0:T(8,128)(2,1)} %hidden_ref.3, f32[1,4096]{1,0:T(1,128)} %scales_ref.5), custom_call_target="tpu_custom_call" | custom-call | bytes 2179076 | tf_op jit(solution)/shard_map/pallas_call | solution.py:28
  21.6 6.8 %collective-permute-start.3 = (bf16[128,2048]{1,0:T(8,128)(2,1)}, bf16[128,2048]{1,0:T(8,128)(2,1)S(1)}, u32[]{:S(2)}, u32[]{:S(2)}) collective-permute-start(bf16[128,2048]{1,0:T(8,128)(2,1)} %get-tuple-element.12), channel_id=1, source_target_pairs={{0,8},{8,0},{1,9},{9,1},{2,10},{10,2},{3,11},{11,3},{4,12},{12,4},... | collective-permute-start | bytes 1572872 | tf_op jit(solution)/shard_map/ppermute | solution.py:158
  28.4 0.0 copy-done.4
  28.4 1.9 %collective-permute-start.1 = (bf16[128,512]{1,0:T(8,128)(2,1)S(1)}, bf16[128,512]{1,0:T(8,128)(2,1)S(1)}, u32[]{:S(2)}, u32[]{:S(2)}) collective-permute-start(bf16[128,512]{1,0:T(8,128)(2,1)S(1)} %copy-done.4), channel_id=1, source_target_pairs={{0,8},{8,0},{1,9},{9,1},{2,10},{10,2},{3,11},{11,3},{4,12},{12,4},... | collective-permute-start | bytes 393224 | tf_op jit(solution)/shard_map/ppermute | solution.py:147
  30.3 6.5 %collective-permute-done.1 = bf16[128,512]{1,0:T(8,128)(2,1)S(1)} collective-permute-done((bf16[128,512]{1,0:T(8,128)(2,1)S(1)}, bf16[128,512]{1,0:T(8,128)(2,1)S(1)}, u32[]{:S(2)}, u32[]{:S(2)}) %collective-permute-start.1) | collective-permute-done | bytes 131104 | tf_op jit(solution)/shard_map/ppermute | solution.py:147
  36.8 0.0 collective-permute-done.3
  36.9 3.1 %convolution_convert_fusion = bf16[2048,512]{1,0:T(8,128)(2,1)} fusion(bf16[128,2048]{1,0:T(8,128)(2,1)S(1)} %collective-permute-done.3, bf16[128,2048]{1,0:T(8,128)(2,1)} %get-tuple-element.11, bf16[128,512]{1,0:T(8,128)(2,1)S(1)} %collective-permute-done.1, bf16[128,512]{1,0:T(8,128)(2,1)S(1)} %copy-done.4), kind=kOutput, calls=%fused_computation | convolution fusion | flops 540540928 | bytes 3407872 | tf_op jit(solution)/shard_map/dot_general | solution.py:159
  40.0 0.0 reduce-scatter.2.cloned.1.call-update
  40.0 2.2 %shard_map.123 = bf16[6,256,128]{2,1,0:T(8,128)(2,1)} custom-call(f32[256,768]{1,0:T(8,128)} %outer_ref.3, f32[256,768]{1,0:T(8,128)} %bitcast.23), custom_call_target="tpu_custom_call" | custom-call | bytes 1966080 | tf_op jit(solution)/shard_map/pallas_call | solution.py:28
  42.2 41.9 %all_to_all.10.spread_ref = bf16[48,32,128]{2,1,0:T(8,128)(2,1)} all-to-all(bf16[48,32,128]{2,1,0:T(8,128)(2,1)} %bitcast.19), channel_id=1, replica_groups=mesh['x_lo'=2,'z'=12,'core'=2,'x_hi'=2,'y_hi'=4,'y_lo'=2] {'x_lo','z','c..., dimensions={0} | all-to-all | bytes 786432 | tf_op jit(solution)/shard_map/all_to_all | solution.py:174
  84.1 1.8 %shard_map.124 = bf16[48,32,128]{2,1,0:T(8,128)(2,1)} custom-call(bf16[48,32,128]{2,1,0:T(8,128)(2,1)} %all_to_all.10.spread_ref), custom_call_target="tpu_custom_call" | custom-call | bytes 786432 | tf_op jit(solution)/shard_map/pallas_call | solution.py:28
  85.9 7.3 %all-to-all-start.1 = ((bf16[48,32,128]{2,1,0:T(8,128)(2,1)}), bf16[48,32,128]{2,1,0:T(8,128)(2,1)S(1)}, u32[]{:S(2)}, u32[]{:S(2)}) async-start(bf16[48,32,128]{2,1,0:T(8,128)(2,1)} %shard_map.124), calls=%async_computation.2 | async-start | bytes 786432 | tf_op jit(solution)/shard_map/all_to_all | solution.py:176
  93.3 0.0 all-gather.2.cloned.1.call-done
  93.3 2.6 %fusion = bf16[128,2048]{1,0:T(8,128)(2,1)S(1)} fusion(bf16[2048,512]{1,0:T(8,128)(2,1)} %all-gather.2.cloned.1.call-done, bf16[128,512]{1,0:T(8,128)(2,1)S(1)} %collective-permute-done.1), kind=kOutput, calls=%fused_computation.3 | convolution fusion | flops 268697600 | bytes 2752512 | tf_op jit(solution)/shard_map/dot_general | solution.py:184
  95.9 4.3 %collective-permute-start.2 = (bf16[128,2048]{1,0:T(8,128)(2,1)S(1)}, bf16[128,2048]{1,0:T(8,128)(2,1)S(1)}, u32[]{:S(2)}, u32[]{:S(2)}) collective-permute-start(bf16[128,2048]{1,0:T(8,128)(2,1)S(1)} %fusion), channel_id=1, source_target_pairs={{0,8},{8,0},{1,9},{9,1},{2,10},{10,2},{3,11},{11,3},{4,12},{12,4},... | collective-permute-start | bytes 1572872 | tf_op jit(solution)/shard_map/ppermute | solution.py:187
  100.3 10.7 %all-to-all-done.1 = bf16[48,32,128]{2,1,0:T(8,128)(2,1)S(1)} async-done(((bf16[48,32,128]{2,1,0:T(8,128)(2,1)}), bf16[48,32,128]{2,1,0:T(8,128)(2,1)S(1)}, u32[]{:S(2)}, u32[]{:S(2)}) %all-to-all-start.1) | async-done | bytes 393248 | tf_op jit(solution)/shard_map/all_to_all | solution.py:176
  111.0 0.7 copy-done.1
  111.7 2.8 %shard_map.125 = (f32[256,768]{1,0:T(8,128)}, f32[256,768]{1,0:T(8,128)}) custom-call(bf16[6,256,128]{2,1,0:T(8,128)(2,1)} %bitcast.18, f32[256,768]{1,0:T(8,128)} %outer_ref.3, f32[256,768]{1,0:T(8,128)} %momentum_ref.1), custom_call_target="tpu_custom_call" | custom-call | bytes 3538944 | tf_op jit(solution)/shard_map/pallas_call | solution.py:28
  114.6 0.0 copy-done
  114.6 2.7 %convolution_bitcast_fusion.own_ref = f32[128,2048]{1,0:T(8,128)} fusion(bf16[2048,512]{1,0:T(8,128)(2,1)S(1)} %copy-done, bf16[128,512]{1,0:T(8,128)(2,1)} %param.10), kind=kOutput, calls=%fused_computation.1 | convolution fusion | flops 268435456 | bytes 3276800 | tf_op jit(solution)/shard_map/dot_general | solution.py:188
  117.2 0.0 collective-permute-done.2.other_ref
  117.2 0.8 copy-done.2
  118.0 4.3 %shard_map.121 = bf16[128,4096]{1,0:T(8,128)(2,1)} custom-call(s32[1]{0:T(128)} %bitcast.upper_ref, bf16[128,4096]{1,0:T(8,128)(2,1)} %hidden_ref.3, bf16[128,4096]{1,0:T(8,128)(2,1)} %res_ref.1, f32[1,4096]{1,0:T(1,128)} %scales_ref.5, f32[128,128]{1,0:T(8,128)} %get-tuple-element.10.inverse_ref, f32[128,2048]{1,0:T(8,128)} %convolution_bitcast_fusion.own_ref, ...), custom_call_target="tpu_custom_call" | custom-call | bytes 4800516 | tf_op jit(solution)/shard_map/pallas_call | solution.py:28
  122.3 2.1 %shard_map.122 = f32[1,256]{1,0:T(1,128)} custom-call(s32[1]{0:T(128)} %bitcast.7.place_ref, bf16[256,512]{1,0:T(8,128)(2,1)} %reduce-scatter.2.cloned.1.call-done.grad_ref, bf16[256,512]{1,0:T(8,128)(2,1)} %bitcast.22, f32[1,4096]{1,0:T(1,128)} %scales_ref.5), custom_call_target="tpu_custom_call" | custom-call | bytes 541700 | tf_op jit(solution)/shard_map/pallas_call | solution.py:28
  (5 shorter events, 0.0 us)
Async XLA Ops:
  8.0 20.4 %copy-start.4 = (bf16[128,512]{1,0:T(8,128)(2,1)S(1)}, bf16[128,512]{1,0:T(8,128)(2,1)}, u32[]{:S(2)}) copy-start(bf16[128,512]{1,0:T(8,128)(2,1)} %param.10) | copy-start | bytes 393220
  8.0 85.3 %all-gather.2.cloned.1.call-start = ((), (), s32[]{:S(2)}) async-start(), calls=%async_computation.3 | async-start | bytes 2621440 | tf_op jit(solution)/shard_map/all_gather | solution.py:146
  8.1 8.0 %collective-permute-start = (bf16[256,512]{1,0:T(8,128)(2,1)}, bf16[256,512]{1,0:T(8,128)(2,1)S(1)}, u32[]{:S(2)}, u32[]{:S(2)}) collective-permute-start(bf16[256,512]{1,0:T(8,128)(2,1)} %bitcast.20), channel_id=1, source_target_pairs={{0,1},{1,0},{2,3},{3,2},{4,5},{5,4},{6,7},{7,6},{8,9},{9,8},{10,11... | collective-permute-start | bytes 786440 | tf_op jit(solution)/shard_map/ppermute | solution.py:141
  16.0 0.7 copy-start.3
  18.6 103.7 %reduce-scatter.2.cloned.1.call-start = ((), (), s32[]{:S(2)}) async-start(), calls=%async_computation.4 | async-start | bytes 2359296 | tf_op jit(solution)/shard_map/reduce_scatter | solution.py:165
  21.6 15.2 %collective-permute-start.3 = (bf16[128,2048]{1,0:T(8,128)(2,1)}, bf16[128,2048]{1,0:T(8,128)(2,1)S(1)}, u32[]{:S(2)}, u32[]{:S(2)}) collective-permute-start(bf16[128,2048]{1,0:T(8,128)(2,1)} %get-tuple-element.12), channel_id=1, source_target_pairs={{0,8},{8,0},{1,9},{9,1},{2,10},{10,2},{3,11},{11,3},{4,12},{12,4},... | collective-permute-start | bytes 1572872 | tf_op jit(solution)/shard_map/ppermute | solution.py:158
  28.4 8.4 %collective-permute-start.1 = (bf16[128,512]{1,0:T(8,128)(2,1)S(1)}, bf16[128,512]{1,0:T(8,128)(2,1)S(1)}, u32[]{:S(2)}, u32[]{:S(2)}) collective-permute-start(bf16[128,512]{1,0:T(8,128)(2,1)S(1)} %copy-done.4), channel_id=1, source_target_pairs={{0,8},{8,0},{1,9},{9,1},{2,10},{10,2},{3,11},{11,3},{4,12},{12,4},... | collective-permute-start | bytes 393224 | tf_op jit(solution)/shard_map/ppermute | solution.py:147
  85.9 25.1 %all-to-all-start.1 = ((bf16[48,32,128]{2,1,0:T(8,128)(2,1)}), bf16[48,32,128]{2,1,0:T(8,128)(2,1)S(1)}, u32[]{:S(2)}, u32[]{:S(2)}) async-start(bf16[48,32,128]{2,1,0:T(8,128)(2,1)} %shard_map.124), calls=%async_computation.2 | async-start | bytes 786432 | tf_op jit(solution)/shard_map/all_to_all | solution.py:176
  93.3 21.3 %copy-start = (bf16[2048,512]{1,0:T(8,128)(2,1)S(1)}, bf16[2048,512]{1,0:T(8,128)(2,1)}, u32[]{:S(2)}) copy-start(bf16[2048,512]{1,0:T(8,128)(2,1)} %all-gather.2.cloned.1.call-done) | copy-start | bytes 6291460
  95.9 21.4 %collective-permute-start.2 = (bf16[128,2048]{1,0:T(8,128)(2,1)S(1)}, bf16[128,2048]{1,0:T(8,128)(2,1)S(1)}, u32[]{:S(2)}, u32[]{:S(2)}) collective-permute-start(bf16[128,2048]{1,0:T(8,128)(2,1)S(1)} %fusion), channel_id=1, source_target_pairs={{0,8},{8,0},{1,9},{9,1},{2,10},{10,2},{3,11},{11,3},{4,12},{12,4},... | collective-permute-start | bytes 1572872 | tf_op jit(solution)/shard_map/ppermute | solution.py:187
  111.0 0.7 copy-start.1
  117.2 0.8 copy-start.2
Sparse Core Ops, SparseCore 0:
  18.7 65.3 all-gather.1
Sparse Core Ops, SparseCore 1:
  40.1 67.4 reduce-scatter.1

commit v6 on v5

--- a/solution.py
+++ b/solution.py
@@ -10,6 +10,7 @@
 REPLICA = AXES[:3]
 FSDP = AXES[3:]
 SWAP = [(0, 1), (1, 0)]
+TWISTED = [[0, 1, 2, 3, 12, 13, 14, 15], [8, 9, 10, 11, 4, 5, 6, 7]]
 f32, bf16 = jnp.float32, jnp.bfloat16
 ROWS = 16
 
@@ -42,28 +43,29 @@
     return lax.rsqrt(jnp.mean(rows * rows, axis=1, keepdims=True) + 1e-05)
 
 
-def pair_kernel(parity_ref, own_ref, other_ref, out_ref):
-    out_ref[parity_ref[0]] = own_ref[...]
-    out_ref[1 - parity_ref[0]] = other_ref[...]
-
-
 def sides(upper_ref, half):
     return [
         pl.ds(pl.multiple_of(side * half, half), half) for side in (upper_ref[0], 1 - upper_ref[0])
     ]
 
 
-def norm_kernel(upper_ref, hidden_ref, scales_ref, kept_ref, sent_ref, inverse_ref):
+def norm_kernel(twist_ref, hidden_ref, scales_ref, kept_ref, sent_ref, inverse_ref):
     tokens, width = hidden_ref.shape
-    own, other = sides(upper_ref, width // 2)
+    part = width // 4
+    pieces = []
+    for target, side in ((sent_ref, 1 - twist_ref[0]), (kept_ref, twist_ref[0])):
+        pieces.append((target, 0, pl.multiple_of(side * 2 * part, part)))
+        pieces.append((target, part, pl.multiple_of((1 - side) * 2 * part + part, part)))
 
     def step(index, _):
         at = pl.ds(pl.multiple_of(index * ROWS, ROWS), ROWS)
         inverse = inverse_of(hidden_ref[at, :].astype(f32))
         inverse_ref[at, :] = jnp.broadcast_to(inverse, (ROWS, 128))
-        for columns, target in ((other, sent_ref), (own, kept_ref)):
+        for target, place, start in pieces:
+            columns = pl.ds(start, part)
             unit = hidden_ref[at, columns].astype(f32) * inverse
-            target[at, :] = (unit * scales_ref[:, columns]).astype(bf16)
+            normed = (unit * scales_ref[:, columns]).astype(bf16)
+            target[at, pl.ds(place, part)] = normed
         return 0
 
     lax.fori_loop(0, tokens // ROWS, step, 0, unroll=2)
@@ -135,15 +137,11 @@
     hidden_in, res_grad, value_grad, value_weight, norm_gain, inner_frag, outer_frag, momentum
 ):
     upper = lax.axis_index("x_hi").reshape(1)
+    twist = lax.bitwise_xor(lax.axis_index("x_hi"), lax.axis_index("y_hi") // 2).reshape(1)
     own_weight = value_weight[0]
     tokens, width = hidden_in.shape
     half = width // 2
-    other_weight = lax.ppermute(own_weight, "y_lo", SWAP)
-    parity = lax.axis_index("y_lo").reshape(1)
-    weight_pair = call(
-        pair_kernel, shape((2, *own_weight.shape), bf16), (parity, own_weight, other_weight)
-    ).reshape(-1, own_weight.shape[1])
-    weight_half = lax.all_gather(weight_pair, "y_hi", axis=0, tiled=True)
+    weight_half = lax.all_gather(own_weight, ("y_hi", "y_lo"), axis=0, tiled=True)
     partner_value = lax.ppermute(value_grad, "x_hi", SWAP)
 
     kept, sent, inverse = call(
@@ -153,7 +151,7 @@
             shape((tokens, half), bf16),
             shape((tokens, 128), f32),
         ),
-        (upper, hidden_in, norm_gain),
+        (twist, hidden_in, norm_gain),
     )
     received = lax.ppermute(sent, "x_hi", SWAP)
     term = lax.dot_general(
@@ -163,7 +161,7 @@
         preferred_element_type=f32,
     ).astype(bf16)
     weight_grad = lax.psum_scatter(
-        term, ("y_hi", "y_lo"), scatter_dimension=0, tiled=True
+        term, FSDP, scatter_dimension=0, tiled=True, axis_index_groups=TWISTED
     )
 
     rows, columns = outer_frag.shape

time: 133 us -> 125 us (0.940)
  starting transfers between devices: 24.5 us -> 20 us
  Pallas kernels: 18.1 us -> 16.2 us
    ppermute x1 -> x0, starting transfers between devices: 4.02 us -> none  [body(): other_weight = lax.ppermute(own_weight, 'y_lo', SWAP)]
    ppermute x1 -> x0, waiting for transfers between devices: 3.95 us -> none  [body(): other_weight = lax.ppermute(own_weight, 'y_lo', SWAP)]
    ppermute x1, waiting for transfers between devices: 0.01 us -> 2.72 us  [body(): other_grad = lax.ppermute(partner_grad, 'x_hi', SWAP)]
    pallas_call x7 -> x6, Pallas kernels: 18.1 us -> 16.2 us  [call(): pl.pallas_call(kernel, out_shape=out_shape, in_specs=[scalar() if a.dtype...]
  transfers between devices with their start and end apart: 7 -> 6, of which waited for: 3 -> 3; matrix products, arithmetic and copies ran while one was open for 6% -> 7% of each run, Pallas kernels for 11% -> 11%
where the time goes in v6:
time: 125 us; the launch traced here: 124 us
  blocking collectives  42.2 us (34%)
  waiting for transfers between devices  20.3 us (16%)
  starting transfers between devices  20 us (16%)
  Pallas kernels  16.2 us (13%)
  between operations  15.6 us (12%)
  matrix products  8.37 us (7%)
  local copies, waits for them, and re-layouts  1.56 us (1%)
    all_to_all x1, blocking collectives, body(): spread = lax.all_to_all(pseudo_grad, REPLICA, 0, 0)  42.2 us
    pallas_call x6, Pallas kernels, call(): pl.pallas_call(kernel, out_shape=out_shape, in_specs=[scalar() if a.dtype...  16.2 us
    all_to_all x1, waiting for transfers between devices, body(): shared = lax.all_to_all(block, REPLICA, 0, 0)  10.6 us
    all_to_all x1, starting transfers between devices, body(): shared = lax.all_to_all(block, REPLICA, 0, 0)  7.8 us
    ppermute x1, waiting for transfers between devices, body(): partner_value = lax.ppermute(value_grad, 'x_hi', SWAP)  6.24 us
    ppermute x1, starting transfers between devices, body(): received = lax.ppermute(sent, 'x_hi', SWAP)  5.46 us
    ppermute x1, starting transfers between devices, body(): other_grad = lax.ppermute(partner_grad, 'x_hi', SWAP)  4.78 us
    dot_general x1, matrix products, body(): lax.dot_general(jnp.concatenate([kept, received], axis=0), jnp.concatenat...  3.13 us
  transfers between devices with their start and end apart: 6, of which 3 were waited for; matrix products, arithmetic and copies ran while one was open for 7% of the time, Pallas kernels for 11%

profile of v6, /device:TPU:1, one launch (start us, length us, event | category | flops | bytes accessed | tf_op | source)
XLA Modules:
  0.0 124.3 jit_solution(5961941621736512397)
XLA Ops:
  8.0 0.0 all-gather.3.cloned.1.call-start
  8.0 0.7 all-gather.3.cloned.1.call-update
  8.7 0.0 reduce-scatter.2.cloned.1.call-start
  8.8 2.9 %shard_map.119 = (bf16[128,2048]{1,0:T(8,128)(2,1)}, bf16[128,2048]{1,0:T(8,128)(2,1)}, f32[128,128]{1,0:T(8,128)}) custom-call(s32[1]{0:T(128)} %bitcast.1.twist_ref, bf16[128,4096]{1,0:T(8,128)(2,1)} %hidden_ref.3, f32[1,4096]{1,0:T(1,128)} %scales_ref.5), custom_call_target="tpu_custom_call" | custom-call | bytes 2179076 | tf_op jit(solution)/shard_map/pallas_call | solution.py:29
  11.7 5.5 %collective-permute-start.2 = (bf16[128,2048]{1,0:T(8,128)(2,1)}, bf16[128,2048]{1,0:T(8,128)(2,1)S(1)}, u32[]{:S(2)}, u32[]{:S(2)}) collective-permute-start(bf16[128,2048]{1,0:T(8,128)(2,1)} %get-tuple-element.12), channel_id=1, source_target_pairs={{0,8},{8,0},{1,9},{9,1},{2,10},{10,2},{3,11},{11,3},{4,12},{12,4},... | collective-permute-start | bytes 1572872 | tf_op jit(solution)/shard_map/ppermute | solution.py:156
  17.2 1.9 %collective-permute-start = (bf16[128,512]{1,0:T(8,128)(2,1)}, bf16[128,512]{1,0:T(8,128)(2,1)S(1)}, u32[]{:S(2)}, u32[]{:S(2)}) collective-permute-start(bf16[128,512]{1,0:T(8,128)(2,1)} %param.10), channel_id=1, source_target_pairs={{0,8},{8,0},{1,9},{9,1},{2,10},{10,2},{3,11},{11,3},{4,12},{12,4},... | collective-permute-start | bytes 393224 | tf_op jit(solution)/shard_map/ppermute | solution.py:145
  19.1 6.2 %collective-permute-done = bf16[128,512]{1,0:T(8,128)(2,1)S(1)} collective-permute-done((bf16[128,512]{1,0:T(8,128)(2,1)}, bf16[128,512]{1,0:T(8,128)(2,1)S(1)}, u32[]{:S(2)}, u32[]{:S(2)}) %collective-permute-start) | collective-permute-done | bytes 131104 | tf_op jit(solution)/shard_map/ppermute | solution.py:145
  25.4 0.0 collective-permute-done.2
  25.4 3.1 %convolution_convert_fusion = bf16[2048,512]{1,0:T(8,128)(2,1)} fusion(bf16[128,2048]{1,0:T(8,128)(2,1)S(1)} %collective-permute-done.2, bf16[128,2048]{1,0:T(8,128)(2,1)} %get-tuple-element.11, bf16[128,512]{1,0:T(8,128)(2,1)S(1)} %collective-permute-done, bf16[128,512]{1,0:T(8,128)(2,1)} %param.10), kind=kOutput, calls=%fused_computation | convolution fusion | flops 540540928 | bytes 3407872 | tf_op jit(solution)/shard_map/dot_general | solution.py:157
  28.5 0.0 reduce-scatter.2.cloned.1.call-update
  28.5 2.2 %shard_map.122 = bf16[6,256,128]{2,1,0:T(8,128)(2,1)} custom-call(f32[256,768]{1,0:T(8,128)} %outer_ref.3, f32[256,768]{1,0:T(8,128)} %bitcast.18), custom_call_target="tpu_custom_call" | custom-call | bytes 1966080 | tf_op jit(solution)/shard_map/pallas_call | solution.py:29
  30.7 42.2 %all_to_all.10.spread_ref = bf16[48,32,128]{2,1,0:T(8,128)(2,1)} all-to-all(bf16[48,32,128]{2,1,0:T(8,128)(2,1)} %bitcast.16), channel_id=1, replica_groups=mesh['x_lo'=2,'z'=12,'core'=2,'x_hi'=2,'y_hi'=4,'y_lo'=2] {'x_lo','z','c..., dimensions={0} | all-to-all | bytes 786432 | tf_op jit(solution)/shard_map/all_to_all | solution.py:172
  72.9 1.8 %shard_map.123 = bf16[48,32,128]{2,1,0:T(8,128)(2,1)} custom-call(bf16[48,32,128]{2,1,0:T(8,128)(2,1)} %all_to_all.10.spread_ref), custom_call_target="tpu_custom_call" | custom-call | bytes 786432 | tf_op jit(solution)/shard_map/pallas_call | solution.py:29
  74.8 7.8 %all-to-all-start.1 = ((bf16[48,32,128]{2,1,0:T(8,128)(2,1)}), bf16[48,32,128]{2,1,0:T(8,128)(2,1)S(1)}, u32[]{:S(2)}, u32[]{:S(2)}) async-start(bf16[48,32,128]{2,1,0:T(8,128)(2,1)} %shard_map.123), calls=%async_computation.2 | async-start | bytes 786432 | tf_op jit(solution)/shard_map/all_to_all | solution.py:174
  82.6 0.0 all-gather.3.cloned.1.call-done
  82.6 0.0 copy-start
  82.6 2.6 %convolution_convert_fusion.1 = bf16[128,2048]{1,0:T(8,128)(2,1)S(1)} fusion(bf16[128,512]{1,0:T(8,128)(2,1)S(1)} %collective-permute-done, bf16[1,2048,512]{2,1,0:T(8,128)(2,1)} %all-gather.3.cloned.1.call-done), kind=kOutput, calls=%fused_computation.1 | convolution fusion | flops 268697600 | bytes 2752512 | tf_op jit(solution)/shard_map/dot_general | solution.py:182
  85.2 4.8 %collective-permute-start.1 = (bf16[128,2048]{1,0:T(8,128)(2,1)S(1)}, bf16[128,2048]{1,0:T(8,128)(2,1)S(1)}, u32[]{:S(2)}, u32[]{:S(2)}) collective-permute-start(bf16[128,2048]{1,0:T(8,128)(2,1)S(1)} %convolution_convert_fusion.1), channel_id=1, source_target_pairs={{0,8},{8,0},{1,9},{9,1},{2,10},{10,2},{3,11},{11,3},{4,12},{12,4},... | collective-permute-start | bytes 1572872 | tf_op jit(solution)/shard_map/ppermute | solution.py:185
  90.0 10.6 %all-to-all-done.1 = bf16[48,32,128]{2,1,0:T(8,128)(2,1)S(1)} async-done(((bf16[48,32,128]{2,1,0:T(8,128)(2,1)}), bf16[48,32,128]{2,1,0:T(8,128)(2,1)S(1)}, u32[]{:S(2)}, u32[]{:S(2)}) %all-to-all-start.1) | async-done | bytes 393248 | tf_op jit(solution)/shard_map/all_to_all | solution.py:174
  100.6 0.0 copy-start.1
  100.6 0.7 copy-done.1
  101.3 2.8 %shard_map.124 = (f32[256,768]{1,0:T(8,128)}, f32[256,768]{1,0:T(8,128)}) custom-call(bf16[6,256,128]{2,1,0:T(8,128)(2,1)} %bitcast.15, f32[256,768]{1,0:T(8,128)} %outer_ref.3, f32[256,768]{1,0:T(8,128)} %momentum_ref.1), custom_call_target="tpu_custom_call" | custom-call | bytes 3538944 | tf_op jit(solution)/shard_map/pallas_call | solution.py:29
  104.1 0.0 copy-done
  104.1 2.7 %fusion.1.own_ref = f32[128,2048]{1,0:T(8,128)} fusion(bf16[128,512]{1,0:T(8,128)(2,1)} %param.10, bf16[1,2048,512]{2,1,0:T(8,128)(2,1)S(1)} %copy-done), kind=kOutput, calls=%fused_computation.3 | convolution fusion | flops 268435456 | bytes 3276800 | tf_op jit(solution)/shard_map/dot_general | solution.py:186
  106.8 2.7 %collective-permute-done.1.other_ref = bf16[128,2048]{1,0:T(8,128)(2,1)S(1)} collective-permute-done((bf16[128,2048]{1,0:T(8,128)(2,1)S(1)}, bf16[128,2048]{1,0:T(8,128)(2,1)S(1)}, u32[]{:S(2)}, u32[]{:S(2)}) %collective-permute-start.1) | collective-permute-done | bytes 524320 | tf_op jit(solution)/shard_map/ppermute | solution.py:185
  109.5 0.0 copy-start.2
  109.5 0.8 copy-done.2
  110.4 4.3 %shard_map.120 = bf16[128,4096]{1,0:T(8,128)(2,1)} custom-call(s32[1]{0:T(128)} %bitcast.upper_ref, bf16[128,4096]{1,0:T(8,128)(2,1)} %hidden_ref.3, bf16[128,4096]{1,0:T(8,128)(2,1)} %res_ref.1, f32[1,4096]{1,0:T(1,128)} %scales_ref.5, f32[128,128]{1,0:T(8,128)} %get-tuple-element.10.inverse_ref, f32[128,2048]{1,0:T(8,128)} %fusion.1.own_ref, ...), custom_call_target="tpu_custom_call" | custom-call | bytes 4800516 | tf_op jit(solution)/shard_map/pallas_call | solution.py:29
  114.7 0.0 reduce-scatter.2.cloned.1.call-done.grad_ref
  114.7 2.1 %shard_map.121 = f32[1,256]{1,0:T(1,128)} custom-call(s32[1]{0:T(128)} %bitcast.4.place_ref, bf16[256,512]{1,0:T(8,128)(2,1)} %reduce-scatter.2.cloned.1.call-done.grad_ref, bf16[256,512]{1,0:T(8,128)(2,1)} %bitcast.17, f32[1,4096]{1,0:T(1,128)} %scales_ref.5), custom_call_target="tpu_custom_call" | custom-call | bytes 541700 | tf_op jit(solution)/shard_map/pallas_call | solution.py:29
Async XLA Ops:
  8.0 74.6 %all-gather.3.cloned.1.call-start = ((), (), s32[]{:S(2)}) async-start(), calls=%async_computation.4 | async-start | bytes 2359296 | tf_op jit(solution)/shard_map/all_gather | solution.py:144
  8.7 105.9 %reduce-scatter.2.cloned.1.call-start = ((), (), s32[]{:S(2)}) async-start(), calls=%async_computation.3 | async-start | bytes 2359296 | tf_op jit(solution)/shard_map/reduce_scatter | solution.py:163
  11.7 13.6 %collective-permute-start.2 = (bf16[128,2048]{1,0:T(8,128)(2,1)}, bf16[128,2048]{1,0:T(8,128)(2,1)S(1)}, u32[]{:S(2)}, u32[]{:S(2)}) collective-permute-start(bf16[128,2048]{1,0:T(8,128)(2,1)} %get-tuple-element.12), channel_id=1, source_target_pairs={{0,8},{8,0},{1,9},{9,1},{2,10},{10,2},{3,11},{11,3},{4,12},{12,4},... | collective-permute-start | bytes 1572872 | tf_op jit(solution)/shard_map/ppermute | solution.py:156
  17.2 8.2 %collective-permute-start = (bf16[128,512]{1,0:T(8,128)(2,1)}, bf16[128,512]{1,0:T(8,128)(2,1)S(1)}, u32[]{:S(2)}, u32[]{:S(2)}) collective-permute-start(bf16[128,512]{1,0:T(8,128)(2,1)} %param.10), channel_id=1, source_target_pairs={{0,8},{8,0},{1,9},{9,1},{2,10},{10,2},{3,11},{11,3},{4,12},{12,4},... | collective-permute-start | bytes 393224 | tf_op jit(solution)/shard_map/ppermute | solution.py:145
  74.8 25.8 %all-to-all-start.1 = ((bf16[48,32,128]{2,1,0:T(8,128)(2,1)}), bf16[48,32,128]{2,1,0:T(8,128)(2,1)S(1)}, u32[]{:S(2)}, u32[]{:S(2)}) async-start(bf16[48,32,128]{2,1,0:T(8,128)(2,1)} %shard_map.123), calls=%async_computation.2 | async-start | bytes 786432 | tf_op jit(solution)/shard_map/all_to_all | solution.py:174
  82.6 21.5 %copy-start = (bf16[1,2048,512]{2,1,0:T(8,128)(2,1)S(1)}, bf16[1,2048,512]{2,1,0:T(8,128)(2,1)}, u32[]{:S(2)}) copy-start(bf16[1,2048,512]{2,1,0:T(8,128)(2,1)} %all-gather.3.cloned.1.call-done) | copy-start | bytes 6291460
  85.2 24.4 %collective-permute-start.1 = (bf16[128,2048]{1,0:T(8,128)(2,1)S(1)}, bf16[128,2048]{1,0:T(8,128)(2,1)S(1)}, u32[]{:S(2)}, u32[]{:S(2)}) collective-permute-start(bf16[128,2048]{1,0:T(8,128)(2,1)S(1)} %convolution_convert_fusion.1), channel_id=1, source_target_pairs={{0,8},{8,0},{1,9},{9,1},{2,10},{10,2},{3,11},{11,3},{4,12},{12,4},... | collective-permute-start | bytes 1572872 | tf_op jit(solution)/shard_map/ppermute | solution.py:185
  100.6 0.7 copy-start.1
  109.5 0.8 copy-start.2
Sparse Core Ops, SparseCore 0:
  11.2 49.4 all-gather.2
Sparse Core Ops, SparseCore 1:
  28.6 66.5 reduce-scatter.1

commit v7 on v5

--- a/solution.py
+++ b/solution.py
@@ -10,6 +10,7 @@
 REPLICA = AXES[:3]
 FSDP = AXES[3:]
 SWAP = [(0, 1), (1, 0)]
+TWISTED = [[0, 1, 2, 3, 12, 13, 14, 15], [8, 9, 10, 11, 4, 5, 6, 7]]
 f32, bf16 = jnp.float32, jnp.bfloat16
 ROWS = 16
 
@@ -42,11 +43,6 @@
     return lax.rsqrt(jnp.mean(rows * rows, axis=1, keepdims=True) + 1e-05)
 
 
-def pair_kernel(parity_ref, own_ref, other_ref, out_ref):
-    out_ref[parity_ref[0]] = own_ref[...]
-    out_ref[1 - parity_ref[0]] = other_ref[...]
-
-
 def sides(upper_ref, half):
     return [
         pl.ds(pl.multiple_of(side * half, half), half) for side in (upper_ref[0], 1 - upper_ref[0])
@@ -95,21 +91,27 @@
 
 
 def hidden_kernel(
-    upper_ref, hidden_ref, res_ref, scales_ref, inverse_ref, own_ref, other_ref, out_ref
+    twist_ref, hidden_ref, res_ref, scales_ref, inverse_ref, own_ref, other_ref, out_ref
 ):
     tokens, width = hidden_ref.shape
-    parts = tuple(zip(sides(upper_ref, width // 2), (own_ref, other_ref)))
+    part = width // 4
+    parts = []
+    for grad_ref, side in ((own_ref, twist_ref[0]), (other_ref, 1 - twist_ref[0])):
+        starts = (side * 2 * part, (1 - side) * 2 * part + part)
+        for place, start in enumerate(starts):
+            columns = pl.ds(pl.multiple_of(start, part), part)
+            parts.append((columns, grad_ref, pl.ds(place * part, part)))
 
     def step(index, _):
         at = pl.ds(pl.multiple_of(index * ROWS, ROWS), ROWS)
         inverse = inverse_ref[at, :][:, :1]
         total = jnp.zeros((ROWS, 1), f32)
-        for columns, grad_ref in parts:
-            scaled = grad_ref[at, :].astype(f32) * scales_ref[:, columns]
+        for columns, grad_ref, place in parts:
+            scaled = grad_ref[at, place].astype(f32) * scales_ref[:, columns]
             total += jnp.sum(scaled * hidden_ref[at, columns].astype(f32), axis=1, keepdims=True)
         shift = inverse * (inverse * total / width)
-        for columns, grad_ref in parts:
-            scaled = grad_ref[at, :].astype(f32) * scales_ref[:, columns]
+        for columns, grad_ref, place in parts:
+            scaled = grad_ref[at, place].astype(f32) * scales_ref[:, columns]
             inner = scaled - hidden_ref[at, columns].astype(f32) * shift
             out_ref[at, columns] = (res_ref[at, columns].astype(f32) + inverse * inner).astype(bf16)
         return 0
@@ -135,15 +137,11 @@
     hidden_in, res_grad, value_grad, value_weight, norm_gain, inner_frag, outer_frag, momentum
 ):
     upper = lax.axis_index("x_hi").reshape(1)
+    twist = lax.bitwise_xor(lax.axis_index("x_hi"), lax.axis_index("y_hi") // 2).reshape(1)
     own_weight = value_weight[0]
     tokens, width = hidden_in.shape
     half = width // 2
-    other_weight = lax.ppermute(own_weight, "y_lo", SWAP)
-    parity = lax.axis_index("y_lo").reshape(1)
-    weight_pair = call(
-        pair_kernel, shape((2, *own_weight.shape), bf16), (parity, own_weight, other_weight)
-    ).reshape(-1, own_weight.shape[1])
-    weight_half = lax.all_gather(weight_pair, "y_hi", axis=0, tiled=True)
+    weight_half = lax.all_gather(own_weight, FSDP, axis=0, tiled=True, axis_index_groups=TWISTED)
     partner_value = lax.ppermute(value_grad, "x_hi", SWAP)
 
     kept, sent, inverse = call(
@@ -189,7 +187,7 @@
     hidden_grad = call(
         hidden_kernel,
         shape(hidden_in.shape, bf16),
-        (upper, hidden_in, res_grad, norm_gain, inverse, own_grad, other_grad),
+        (twist, hidden_in, res_grad, norm_gain, inverse, own_grad, other_grad),
     )
 
     gain_grad = call(

time: 133 us -> 128 us (0.962)
  the two profiles are of different devices: /device:TPU:1 before, /device:TPU:37 now
where the time goes in v7:
time: 128 us; the launch traced here: 127 us
  blocking collectives  43.1 us (34%)
  waiting for transfers between devices  26.3 us (21%)
  Pallas kernels  16.3 us (13%)
  starting transfers between devices  16.1 us (13%)
  between operations  15.6 us (12%)
  matrix products  8.38 us (7%)
  local copies, waits for them, and re-layouts  1.56 us (1%)
    all_to_all x1, blocking collectives, body(): spread = lax.all_to_all(pseudo_grad, REPLICA, 0, 0)  43.1 us
    pallas_call x6, Pallas kernels, call(): pl.pallas_call(kernel, out_shape=out_shape, in_specs=[scalar() if a.dtype...  16.3 us
    all_to_all x1, waiting for transfers between devices, body(): shared = lax.all_to_all(block, REPLICA, 0, 0)  13.2 us
    ppermute x1, waiting for transfers between devices, body(): partner_value = lax.ppermute(value_grad, 'x_hi', SWAP)  12.4 us
    all_to_all x1, starting transfers between devices, body(): shared = lax.all_to_all(block, REPLICA, 0, 0)  7.34 us
    ppermute x1, starting transfers between devices, body(): partner_value = lax.ppermute(value_grad, 'x_hi', SWAP)  4.65 us
    dot_general x1, matrix products, body(): lax.dot_general(jnp.concatenate([kept, received], axis=0), jnp.concatenat...  3.13 us
    dot_general x1, matrix products, body(): lax.dot_general(value_grad, weight_half, rows_by_rows, preferred_element_...  2.68 us
  transfers between devices with their start and end apart: 6, of which 2 were waited for; matrix products, arithmetic and copies ran while one was open for 7% of the time, Pallas kernels for 11%

profile of v7, /device:TPU:37, one launch (start us, length us, event | category | flops | bytes accessed | tf_op | source)
XLA Modules:
  0.0 127.4 jit_solution(4798871794678447526)
XLA Ops:
  8.0 0.0 all-gather.3.cloned.1.call-start
  8.0 0.7 all-gather.3.cloned.1.call-update
  8.7 0.0 reduce-scatter.2.cloned.1.call-start
  8.8 2.9 %shard_map.119 = (bf16[128,2048]{1,0:T(8,128)(2,1)}, bf16[128,2048]{1,0:T(8,128)(2,1)}, f32[128,128]{1,0:T(8,128)}) custom-call(s32[1]{0:T(128)} %bitcast.1.upper_ref, bf16[128,4096]{1,0:T(8,128)(2,1)} %hidden_ref.3, f32[1,4096]{1,0:T(1,128)} %scales_ref.5), custom_call_target="tpu_custom_call" | custom-call | bytes 2179076 | tf_op jit(solution)/shard_map/pallas_call | solution.py:29
  11.7 2.1 %collective-permute-start.2 = (bf16[128,2048]{1,0:T(8,128)(2,1)}, bf16[128,2048]{1,0:T(8,128)(2,1)S(1)}, u32[]{:S(2)}, u32[]{:S(2)}) collective-permute-start(bf16[128,2048]{1,0:T(8,128)(2,1)} %get-tuple-element.12), channel_id=1, source_target_pairs={{0,8},{8,0},{1,9},{9,1},{2,10},{10,2},{3,11},{11,3},{4,12},{12,4},... | collective-permute-start | bytes 1572872 | tf_op jit(solution)/shard_map/ppermute | solution.py:156
  13.9 4.7 %collective-permute-start = (bf16[128,512]{1,0:T(8,128)(2,1)}, bf16[128,512]{1,0:T(8,128)(2,1)S(1)}, u32[]{:S(2)}, u32[]{:S(2)}) collective-permute-start(bf16[128,512]{1,0:T(8,128)(2,1)} %param.10), channel_id=1, source_target_pairs={{0,8},{8,0},{1,9},{9,1},{2,10},{10,2},{3,11},{11,3},{4,12},{12,4},... | collective-permute-start | bytes 393224 | tf_op jit(solution)/shard_map/ppermute | solution.py:145
  18.5 12.4 %collective-permute-done = bf16[128,512]{1,0:T(8,128)(2,1)S(1)} collective-permute-done((bf16[128,512]{1,0:T(8,128)(2,1)}, bf16[128,512]{1,0:T(8,128)(2,1)S(1)}, u32[]{:S(2)}, u32[]{:S(2)}) %collective-permute-start) | collective-permute-done | bytes 131104 | tf_op jit(solution)/shard_map/ppermute | solution.py:145
  30.9 0.0 collective-permute-done.2
  30.9 3.1 %convolution_convert_fusion = bf16[2048,512]{1,0:T(8,128)(2,1)} fusion(bf16[128,2048]{1,0:T(8,128)(2,1)S(1)} %collective-permute-done.2, bf16[128,2048]{1,0:T(8,128)(2,1)} %get-tuple-element.11, bf16[128,512]{1,0:T(8,128)(2,1)S(1)} %collective-permute-done, bf16[128,512]{1,0:T(8,128)(2,1)} %param.10), kind=kOutput, calls=%fused_computation | convolution fusion | flops 540540928 | bytes 3407872 | tf_op jit(solution)/shard_map/dot_general | solution.py:157
  34.1 0.0 reduce-scatter.2.cloned.1.call-update
  34.1 2.2 %shard_map.122 = bf16[6,256,128]{2,1,0:T(8,128)(2,1)} custom-call(f32[256,768]{1,0:T(8,128)} %outer_ref.3, f32[256,768]{1,0:T(8,128)} %bitcast.18), custom_call_target="tpu_custom_call" | custom-call | bytes 1966080 | tf_op jit(solution)/shard_map/pallas_call | solution.py:29
  36.4 43.1 %all_to_all.10.spread_ref = bf16[48,32,128]{2,1,0:T(8,128)(2,1)} all-to-all(bf16[48,32,128]{2,1,0:T(8,128)(2,1)} %bitcast.16), channel_id=1, replica_groups=mesh['x_lo'=2,'z'=12,'core'=2,'x_hi'=2,'y_hi'=4,'y_lo'=2] {'x_lo','z','c..., dimensions={0} | all-to-all | bytes 786432 | tf_op jit(solution)/shard_map/all_to_all | solution.py:172
  79.5 1.8 %shard_map.123 = bf16[48,32,128]{2,1,0:T(8,128)(2,1)} custom-call(bf16[48,32,128]{2,1,0:T(8,128)(2,1)} %all_to_all.10.spread_ref), custom_call_target="tpu_custom_call" | custom-call | bytes 786432 | tf_op jit(solution)/shard_map/pallas_call | solution.py:29
  81.3 7.3 %all-to-all-start.1 = ((bf16[48,32,128]{2,1,0:T(8,128)(2,1)}), bf16[48,32,128]{2,1,0:T(8,128)(2,1)S(1)}, u32[]{:S(2)}, u32[]{:S(2)}) async-start(bf16[48,32,128]{2,1,0:T(8,128)(2,1)} %shard_map.123), calls=%async_computation.2 | async-start | bytes 786432 | tf_op jit(solution)/shard_map/all_to_all | solution.py:174
  88.7 0.0 all-gather.3.cloned.1.call-done
  88.7 0.0 copy-start
  88.7 2.6 %convolution_convert_fusion.1 = bf16[128,2048]{1,0:T(8,128)(2,1)S(1)} fusion(bf16[128,512]{1,0:T(8,128)(2,1)S(1)} %collective-permute-done, bf16[1,2048,512]{2,1,0:T(8,128)(2,1)} %all-gather.3.cloned.1.call-done), kind=kOutput, calls=%fused_computation.1 | convolution fusion | flops 268697600 | bytes 2752512 | tf_op jit(solution)/shard_map/dot_general | solution.py:182
  91.3 1.9 %collective-permute-start.1 = (bf16[128,2048]{1,0:T(8,128)(2,1)S(1)}, bf16[128,2048]{1,0:T(8,128)(2,1)S(1)}, u32[]{:S(2)}, u32[]{:S(2)}) collective-permute-start(bf16[128,2048]{1,0:T(8,128)(2,1)S(1)} %convolution_convert_fusion.1), channel_id=1, source_target_pairs={{0,8},{8,0},{1,9},{9,1},{2,10},{10,2},{3,11},{11,3},{4,12},{12,4},... | collective-permute-start | bytes 1572872 | tf_op jit(solution)/shard_map/ppermute | solution.py:185
  93.2 13.2 %all-to-all-done.1 = bf16[48,32,128]{2,1,0:T(8,128)(2,1)S(1)} async-done(((bf16[48,32,128]{2,1,0:T(8,128)(2,1)}), bf16[48,32,128]{2,1,0:T(8,128)(2,1)S(1)}, u32[]{:S(2)}, u32[]{:S(2)}) %all-to-all-start.1) | async-done | bytes 393248 | tf_op jit(solution)/shard_map/all_to_all | solution.py:174
  106.4 0.0 copy-start.1
  106.4 0.7 copy-done.1
  107.1 2.8 %shard_map.124 = (f32[256,768]{1,0:T(8,128)}, f32[256,768]{1,0:T(8,128)}) custom-call(bf16[6,256,128]{2,1,0:T(8,128)(2,1)} %bitcast.15, f32[256,768]{1,0:T(8,128)} %outer_ref.3, f32[256,768]{1,0:T(8,128)} %momentum_ref.1), custom_call_target="tpu_custom_call" | custom-call | bytes 3538944 | tf_op jit(solution)/shard_map/pallas_call | solution.py:29
  109.9 0.0 copy-done
  109.9 2.7 %fusion.1.own_ref = f32[128,2048]{1,0:T(8,128)} fusion(bf16[128,512]{1,0:T(8,128)(2,1)} %param.10, bf16[1,2048,512]{2,1,0:T(8,128)(2,1)S(1)} %copy-done), kind=kOutput, calls=%fused_computation.3 | convolution fusion | flops 268435456 | bytes 3276800 | tf_op jit(solution)/shard_map/dot_general | solution.py:186
  112.6 0.0 collective-permute-done.1.other_ref
  112.6 0.0 copy-start.2
  112.6 0.8 copy-done.2
  113.5 4.3 %shard_map.120 = bf16[128,4096]{1,0:T(8,128)(2,1)} custom-call(s32[1]{0:T(128)} %bitcast.twist_ref, bf16[128,4096]{1,0:T(8,128)(2,1)} %hidden_ref.3, bf16[128,4096]{1,0:T(8,128)(2,1)} %res_ref.1, f32[1,4096]{1,0:T(1,128)} %scales_ref.5, f32[128,128]{1,0:T(8,128)} %get-tuple-element.10.inverse_ref, f32[128,2048]{1,0:T(8,128)} %fusion.1.own_ref, ...), custom_call_target="tpu_custom_call" | custom-call | bytes 4800516 | tf_op jit(solution)/shard_map/pallas_call | solution.py:29
  117.8 0.0 reduce-scatter.2.cloned.1.call-done.grad_ref
  117.8 2.1 %shard_map.121 = f32[1,256]{1,0:T(1,128)} custom-call(s32[1]{0:T(128)} %bitcast.4.place_ref, bf16[256,512]{1,0:T(8,128)(2,1)} %reduce-scatter.2.cloned.1.call-done.grad_ref, bf16[256,512]{1,0:T(8,128)(2,1)} %bitcast.17, f32[1,4096]{1,0:T(1,128)} %scales_ref.5), custom_call_target="tpu_custom_call" | custom-call | bytes 541700 | tf_op jit(solution)/shard_map/pallas_call | solution.py:29
Async XLA Ops:
  8.0 80.7 %all-gather.3.cloned.1.call-start = ((), (), s32[]{:S(2)}) async-start(), calls=%async_computation.4 | async-start | bytes 2359296 | tf_op jit(solution)/shard_map/all_gather | solution.py:144
  8.7 109.1 %reduce-scatter.2.cloned.1.call-start = ((), (), s32[]{:S(2)}) async-start(), calls=%async_computation.3 | async-start | bytes 2359296 | tf_op jit(solution)/shard_map/reduce_scatter | solution.py:163
  11.7 19.2 %collective-permute-start.2 = (bf16[128,2048]{1,0:T(8,128)(2,1)}, bf16[128,2048]{1,0:T(8,128)(2,1)S(1)}, u32[]{:S(2)}, u32[]{:S(2)}) collective-permute-start(bf16[128,2048]{1,0:T(8,128)(2,1)} %get-tuple-element.12), channel_id=1, source_target_pairs={{0,8},{8,0},{1,9},{9,1},{2,10},{10,2},{3,11},{11,3},{4,12},{12,4},... | collective-permute-start | bytes 1572872 | tf_op jit(solution)/shard_map/ppermute | solution.py:156
  13.9 17.1 %collective-permute-start = (bf16[128,512]{1,0:T(8,128)(2,1)}, bf16[128,512]{1,0:T(8,128)(2,1)S(1)}, u32[]{:S(2)}, u32[]{:S(2)}) collective-permute-start(bf16[128,512]{1,0:T(8,128)(2,1)} %param.10), channel_id=1, source_target_pairs={{0,8},{8,0},{1,9},{9,1},{2,10},{10,2},{3,11},{11,3},{4,12},{12,4},... | collective-permute-start | bytes 393224 | tf_op jit(solution)/shard_map/ppermute | solution.py:145
  81.3 25.1 %all-to-all-start.1 = ((bf16[48,32,128]{2,1,0:T(8,128)(2,1)}), bf16[48,32,128]{2,1,0:T(8,128)(2,1)S(1)}, u32[]{:S(2)}, u32[]{:S(2)}) async-start(bf16[48,32,128]{2,1,0:T(8,128)(2,1)} %shard_map.123), calls=%async_computation.2 | async-start | bytes 786432 | tf_op jit(solution)/shard_map/all_to_all | solution.py:174
  88.7 21.3 %copy-start = (bf16[1,2048,512]{2,1,0:T(8,128)(2,1)S(1)}, bf16[1,2048,512]{2,1,0:T(8,128)(2,1)}, u32[]{:S(2)}) copy-start(bf16[1,2048,512]{2,1,0:T(8,128)(2,1)} %all-gather.3.cloned.1.call-done) | copy-start | bytes 6291460
  91.3 21.4 %collective-permute-start.1 = (bf16[128,2048]{1,0:T(8,128)(2,1)S(1)}, bf16[128,2048]{1,0:T(8,128)(2,1)S(1)}, u32[]{:S(2)}, u32[]{:S(2)}) collective-permute-start(bf16[128,2048]{1,0:T(8,128)(2,1)S(1)} %convolution_convert_fusion.1), channel_id=1, source_target_pairs={{0,8},{8,0},{1,9},{9,1},{2,10},{10,2},{3,11},{11,3},{4,12},{12,4},... | collective-permute-start | bytes 1572872 | tf_op jit(solution)/shard_map/ppermute | solution.py:185
  106.4 0.7 copy-start.1
  112.6 0.8 copy-start.2
Sparse Core Ops, SparseCore 0:
  11.2 52.4 all-gather.2
Sparse Core Ops, SparseCore 1:
  34.2 58.2 reduce-scatter.1
